TPU v7x, 256 devices: a whole 4x4x8 slice. The times are simulated.
256 devices in a mesh: ctx: 64 (over z, y_hi, x), tp: 4 (over y_lo, core).
Axes of the slice: x: 4, y: 4 (y_hi: 2, y_lo: 2; y = y_hi * 2 + y_lo), z: 8, core: 2. Of those that a mesh axis runs over, the one named last changes fastest.
Arguments:
- queries: bfloat16 [16384, 2560], P('ctx', 'tp'), may hold values from -6 to 6
- keys: bfloat16 [16384, 512], P('ctx', 'tp'), may hold values from -6 to 6
- values: bfloat16 [16384, 512], P('ctx', 'tp'), may hold values from -6 to 6
- out_weight: bfloat16 [2560, 5120], P('tp'), may hold values from -0.125 to 0.125
- cotangent: bfloat16 [16384, 5120], P('ctx', 'tp'), may hold values from -6 to 6
- doc_ids: int32 [128], replicated, may hold values from 0 to 15, never falling along the last dimension, each value on 1 to 16 neighbouring positions
Outputs:
- mixed: bfloat16 [16384, 5120], P('ctx', 'tp')
- grad_queries: bfloat16 [16384, 2560], P('ctx', 'tp')
- keys_gradient: bfloat16 [16384, 512], P('ctx', 'tp')
- values_gradient: bfloat16 [16384, 512], P('ctx', 'tp')
Inputs may be any that keep to these rules, and one draw needn't show every extreme that they name: `doc_ids`: ids never fall from one block to the next; each document covers 1 to 16 blocks and one covers exactly 16.
All inputs are finite; a program needn't handle non-finite values.
Results may differ from a plain program's by a relative error of at most 0.033.
Values may be sent and summed in bfloat16 or wider, within the bound.
A program may use at most 128 MiB of HBM per device.

v0:
```python
import math

import jax
import jax.numpy as jnp
from jax import lax
from jax.sharding import PartitionSpec as P

HEAD_SIZE = 128
BLK = 128


NEG_FILL = -1e30


def from_behind(array, axis, by):
    devices = lax.axis_size(axis)
    pairs = [(i, i + by) for i in range(devices) if 0 <= i + by < devices]
    return lax.ppermute(array, axis, pairs)


def from_behind_2(array, axis, by):
    devices = lax.axis_size(axis)
    return lax.ppermute(array, axis, [(i, (i + by) % devices) for i in range(devices)])


def doc_span(doc_ids, leading_row, count):
    blocks = lax.dynamic_slice_in_dim(doc_ids, leading_row // BLK, count // BLK, 0)
    return jnp.repeat(blocks, BLK, total_repeat_length=count)


def allowed_pairs(doc_ids, query_first, query_count, key_first, key_count, valid):
    query_pos = query_first + lax.iota(jnp.int32, query_count)
    key_pos = key_first + lax.iota(jnp.int32, key_count)
    same_doc = (
        doc_span(doc_ids, query_first, query_count)[:, None]
        == doc_span(doc_ids, key_first, key_count)[None, :]
    )
    return same_doc & (key_pos[None, :] <= query_pos[:, None]) & valid


def on_device(queries, keys, values, out_weight, cotangent, doc_ids):
    row_count = queries.shape[0]
    key_heads = keys.shape[1] // HEAD_SIZE
    query_heads = queries.shape[1] // HEAD_SIZE
    query_group_width = query_heads // key_heads
    key_width = key_heads * HEAD_SIZE
    score_scale = 1.0 / math.sqrt(HEAD_SIZE)
    ctx_count = lax.axis_size("ctx")
    my_index = lax.axis_index("ctx")
    query_first = my_index * row_count
    block_total = row_count * ctx_count // BLK
    doc_most = min(8 * row_count // BLK, block_total // 2)
    reach = min((doc_most * BLK - 1) // row_count + 1, ctx_count - 1)
    query_view = queries.reshape(row_count, key_heads, query_group_width, HEAD_SIZE)
    key_value = jnp.concatenate([keys, values], axis=1)
    steps_ahead = jnp.arange(1, reach + 1, dtype=jnp.int32)

    def split_keys(sub_block):
        block_rows = sub_block.shape[0]
        key_block = sub_block[:, :key_width].reshape(block_rows, key_heads, HEAD_SIZE)
        value_block = sub_block[:, key_width:].reshape(block_rows, key_heads, HEAD_SIZE)
        return (key_block, value_block)

    def sweep(shard_rows, leading_row, visit, carried, valid):
        piece_rows = shard_rows.shape[0]
        block_width = math.gcd(piece_rows, 1024)

        def one_step(step_index, running):
            offset = step_index * block_width
            return visit(running, shard_rows, leading_row + offset, offset, valid)

        return lax.fori_loop(0, piece_rows // block_width, one_step, carried)

    def forward_block(carried, sub_block, key_first, offset, valid):
        key_block, value_block = split_keys(sub_block)
        allowed = allowed_pairs(
            doc_ids, query_first, row_count, key_first, sub_block.shape[0], valid
        )
        row_top, row_total, weighted = carried
        scores = (
            jnp.einsum("tkgd,nkd->kgtn", query_view, key_block, preferred_element_type=jnp.float32)
            * score_scale
        )
        scores = jnp.where(allowed, scores, NEG_FILL)
        new_top = jnp.maximum(row_top, jnp.max(scores, axis=-1))
        factor = jnp.exp(row_top - new_top)
        exp_terms = jnp.where(allowed, jnp.exp(scores - new_top[..., None]), 0.0)
        row_total = row_total * factor + jnp.sum(exp_terms, axis=-1)
        weighted = weighted * factor[..., None] + jnp.einsum(
            "kgtn,nkd->kgtd",
            exp_terms.astype(jnp.bfloat16),
            value_block,
            preferred_element_type=jnp.float32,
        )
        return (new_top, row_total, weighted)

    start_state = (
        jnp.full((key_heads, query_group_width, row_count), NEG_FILL, jnp.float32),
        jnp.zeros((key_heads, query_group_width, row_count), jnp.float32),
        jnp.zeros((key_heads, query_group_width, row_count, HEAD_SIZE), jnp.float32),
    )
    state = sweep(key_value, query_first, forward_block, start_state, True)

    def forward_step(carry, step):
        key_now, running = carry
        key_next = from_behind(key_now, "ctx", 1)
        source = my_index - step
        running = sweep(key_next, source * row_count, forward_block, running, source >= 0)
        return ((key_next, running), key_next)

    (key_last, state), key_stack = lax.scan(forward_step, (key_value, state), steps_ahead)
    row_top, row_total, weighted = state
    lse = row_top + jnp.log(row_total)
    attn_heads = weighted / row_total[..., None]
    attn = (
        jnp.transpose(attn_heads, (2, 0, 1, 3))
        .reshape(row_count, query_heads * HEAD_SIZE)
        .astype(jnp.bfloat16)
    )
    partial_out = jnp.dot(attn, out_weight, preferred_element_type=jnp.float32)
    mixed = lax.psum_scatter(
        partial_out.astype(jnp.bfloat16), "tp", scatter_dimension=1, tiled=True
    )
    attention_gradient = lax.dot_general(
        lax.all_gather(cotangent, "tp", axis=1, tiled=True),
        out_weight,
        (((1,), (1,)), ((), ())),
        preferred_element_type=jnp.float32,
    ).astype(jnp.bfloat16)
    grad_view = attention_gradient.reshape(row_count, key_heads, query_group_width, HEAD_SIZE)
    attn_view = attn.astype(jnp.float32).reshape(row_count, key_heads, query_group_width, HEAD_SIZE)
    delta = jnp.transpose(jnp.sum(grad_view.astype(jnp.float32) * attn_view, axis=-1), (1, 2, 0))

    def backward_block(carried, sub_block, key_first, offset, valid):
        key_block, value_block = split_keys(sub_block)
        block_rows = sub_block.shape[0]
        allowed = allowed_pairs(doc_ids, query_first, row_count, key_first, block_rows, valid)
        query_sum, key_grads = carried
        scores = (
            jnp.einsum("tkgd,nkd->kgtn", query_view, key_block, preferred_element_type=jnp.float32)
            * score_scale
        )
        scores = jnp.where(allowed, scores, NEG_FILL)
        probs = jnp.where(allowed, jnp.exp(scores - lse[..., None]), 0.0)
        weights = probs.astype(jnp.bfloat16)
        value_grad = jnp.einsum(
            "kgtn,tkgd->nkd", weights, grad_view, preferred_element_type=jnp.float32
        )
        prob_grad = jnp.einsum(
            "tkgd,nkd->kgtn", grad_view, value_block, preferred_element_type=jnp.float32
        )
        score_grad = (probs * (prob_grad - delta[..., None])).astype(jnp.bfloat16)
        query_grad = (
            jnp.einsum("kgtn,nkd->kgtd", score_grad, key_block, preferred_element_type=jnp.float32)
            * score_scale
        )
        key_grad = (
            jnp.einsum("kgtn,tkgd->nkd", score_grad, query_view, preferred_element_type=jnp.float32)
            * score_scale
        )
        fresh = jnp.concatenate(
            [key_grad.reshape(block_rows, key_width), value_grad.reshape(block_rows, key_width)],
            axis=1,
        )
        earlier = key_grads
        key_grads = earlier + fresh
        return (query_sum + query_grad, key_grads)

    query_zero = jnp.zeros((key_heads, query_group_width, row_count, HEAD_SIZE), jnp.float32)
    grad_start = jnp.zeros((row_count, 2 * key_width), jnp.float32)
    query_sum, own_grads = sweep(
        key_value, query_first, backward_block, (query_zero, grad_start), True
    )

    def carry_step(carry, step):
        key_now, grad_now, running = carry
        key_next = from_behind(key_now, "ctx", 1)
        grad_next = from_behind_2(grad_now.astype(jnp.bfloat16), "ctx", 1).astype(grad_now.dtype)
        source = my_index - step
        running, grad_next = sweep(
            key_next, source * row_count, backward_block, (running, grad_next), source >= 0
        )
        return ((key_next, grad_next, running), None)

    (key_end, grad_end, query_sum), unused = lax.scan(
        carry_step, (key_value, own_grads, query_sum), steps_ahead
    )
    grad_pairs = from_behind_2(grad_end.astype(jnp.bfloat16), "ctx", -reach).astype(grad_end.dtype)
    grad_queries = (
        jnp.transpose(query_sum, (2, 0, 1, 3))
        .reshape(row_count, query_heads * HEAD_SIZE)
        .astype(jnp.bfloat16)
    )
    keys_gradient = grad_pairs[:, :key_width].astype(jnp.bfloat16)
    values_gradient = grad_pairs[:, key_width:].astype(jnp.bfloat16)
    return (mixed, grad_queries, keys_gradient, values_gradient)


def solution(mesh):
    return jax.shard_map(
        on_device,
        mesh=mesh,
        in_specs=(
            P("ctx", "tp"),
            P("ctx", "tp"),
            P("ctx", "tp"),
            P("tp", None),
            P("ctx", "tp"),
            P(),
        ),
        out_specs=(P("ctx", "tp"), P("ctx", "tp"), P("ctx", "tp"), P("ctx", "tp")),
        check_vma=False,
    )
```

profile of v0, /device:TPU:96, one launch (start us, length us, event | category | flops | bytes accessed | tf_op | source)
XLA Modules:
  0.0 277.2 jit_solution(5624273176631988695)
XLA Ops:
  7.2 0.7 all-gather.2.cloned.1.call-update
  8.0 0.7 dynamic_slice.49
  9.3 1.1 copy.37
  10.5 1.2 and_select_fusion
  13.6 101.7 %while.38 = (s32[]{:T(128)}, bf16[256,256]{1,0:T(8,128)(2,1)S(1)}, f32[1,5,256]{2,1,0:T(8,128)S(1)}, f32[1,5,256]{2,1,0:T(8,128)S(1)}, f32[1,5,256,128]{3,2,1,0:...) while((s32[]{:T(128)}, bf16[256,256]{1,0:T(8,128)(2,1)S(1)}, ...), condition=%wide.region_5.7_spmd, body=%wide.region_2.6_spmd.sunk | while | flops 171318816 | bytes 6846975 | solution.py:111
  13.6 3.4 %collective-permute-start = (bf16[256,256]{1,0:T(8,128)(2,1)S(1)}, bf16[256,256]{1,0:T(8,128)(2,1)S(1)}, u32[]{:S(2)}, u32[]{:S(2)}) collective-permute-start(bf16[256,256]{1,0:T(8,128)(2,1)S(1)} %get-tuple-element.1088), channel_id=1, source_target_pairs={{0,4},{4,8},{8,12},{12,16},{16,20},{20,24},{24,28},{28,32},{32,36}... | collective-permute-start | bytes 393224 | tf_op jit(solution)/shard_map/while/body/eval_jaxpr/ppermute | solution.py:18
  19.5 2.5 select_select_fusion.6
  22.2 3.1 %collective-permute-done = bf16[256,256]{1,0:T(8,128)(2,1)S(1)} collective-permute-done((bf16[256,256]{1,0:T(8,128)(2,1)S(1)}, bf16[256,256]{1,0:T(8,128)(2,1)S(1)}, u32[]{:S(2)}, u32[]{:S(2)}) %collective-permute-start) | collective-permute-done | bytes 131104 | tf_op jit(solution)/shard_map/while/body/eval_jaxpr/ppermute | solution.py:18
  26.5 1.9 collective-permute-start
  31.0 2.5 select_select_fusion.6
  33.6 4.4 %collective-permute-done = bf16[256,256]{1,0:T(8,128)(2,1)S(1)} collective-permute-done((bf16[256,256]{1,0:T(8,128)(2,1)S(1)}, bf16[256,256]{1,0:T(8,128)(2,1)S(1)}, u32[]{:S(2)}, u32[]{:S(2)}) %collective-permute-start) | collective-permute-done | bytes 131104 | tf_op jit(solution)/shard_map/while/body/eval_jaxpr/ppermute | solution.py:18
  39.3 1.9 collective-permute-start
  43.7 2.5 select_select_fusion.6
  46.4 4.4 %collective-permute-done = bf16[256,256]{1,0:T(8,128)(2,1)S(1)} collective-permute-done((bf16[256,256]{1,0:T(8,128)(2,1)S(1)}, bf16[256,256]{1,0:T(8,128)(2,1)S(1)}, u32[]{:S(2)}, u32[]{:S(2)}) %collective-permute-start) | collective-permute-done | bytes 131104 | tf_op jit(solution)/shard_map/while/body/eval_jaxpr/ppermute | solution.py:18
  52.0 1.9 collective-permute-start
  55.9 0.6 fusion.97
  56.5 2.5 select_select_fusion.6
  59.1 4.3 %collective-permute-done = bf16[256,256]{1,0:T(8,128)(2,1)S(1)} collective-permute-done((bf16[256,256]{1,0:T(8,128)(2,1)S(1)}, bf16[256,256]{1,0:T(8,128)(2,1)S(1)}, u32[]{:S(2)}, u32[]{:S(2)}) %collective-permute-start) | collective-permute-done | bytes 131104 | tf_op jit(solution)/shard_map/while/body/eval_jaxpr/ppermute | solution.py:18
  64.7 1.9 collective-permute-start
  68.6 0.6 fusion.97
  69.2 2.5 select_select_fusion.6
  71.8 4.3 %collective-permute-done = bf16[256,256]{1,0:T(8,128)(2,1)S(1)} collective-permute-done((bf16[256,256]{1,0:T(8,128)(2,1)S(1)}, bf16[256,256]{1,0:T(8,128)(2,1)S(1)}, u32[]{:S(2)}, u32[]{:S(2)}) %collective-permute-start) | collective-permute-done | bytes 131104 | tf_op jit(solution)/shard_map/while/body/eval_jaxpr/ppermute | solution.py:18
  77.4 1.9 collective-permute-start
  81.8 2.5 select_select_fusion.6
  84.5 4.3 %collective-permute-done = bf16[256,256]{1,0:T(8,128)(2,1)S(1)} collective-permute-done((bf16[256,256]{1,0:T(8,128)(2,1)S(1)}, bf16[256,256]{1,0:T(8,128)(2,1)S(1)}, u32[]{:S(2)}, u32[]{:S(2)}) %collective-permute-start) | collective-permute-done | bytes 131104 | tf_op jit(solution)/shard_map/while/body/eval_jaxpr/ppermute | solution.py:18
  90.0 1.9 collective-permute-start
  94.5 2.5 select_select_fusion.6
  97.1 4.3 %collective-permute-done = bf16[256,256]{1,0:T(8,128)(2,1)S(1)} collective-permute-done((bf16[256,256]{1,0:T(8,128)(2,1)S(1)}, bf16[256,256]{1,0:T(8,128)(2,1)S(1)}, u32[]{:S(2)}, u32[]{:S(2)}) %collective-permute-start) | collective-permute-done | bytes 131104 | tf_op jit(solution)/shard_map/while/body/eval_jaxpr/ppermute | solution.py:18
  102.7 1.9 collective-permute-start
  107.1 2.5 select_select_fusion.6
  109.8 4.3 %collective-permute-done = bf16[256,256]{1,0:T(8,128)(2,1)S(1)} collective-permute-done((bf16[256,256]{1,0:T(8,128)(2,1)S(1)}, bf16[256,256]{1,0:T(8,128)(2,1)S(1)}, u32[]{:S(2)}, u32[]{:S(2)}) %collective-permute-start) | collective-permute-done | bytes 131104 | tf_op jit(solution)/shard_map/while/body/eval_jaxpr/ppermute | solution.py:18
  115.6 5.9 %convolution_convert_fusion.1 = bf16[256,640]{1,0:T(8,128)(2,1)S(1)} fusion(bf16[256,5120]{1,0:T(8,128)(2,1)} %all-gather.2.cloned.1.call-done, bf16[640,5120]{1,0:T(8,128)(2,1)} %param.31), kind=kOutput, calls=%fused_computation.74 | convolution fusion | flops 1677885440 | bytes 9502720 | tf_op jit(solution)/shard_map/dot_general | solution.py:124
  123.4 6.6 %convolution_convert_fusion = bf16[256,5120]{1,0:T(8,128)(2,1)} fusion(bf16[256,640]{0,1:T(8,128)(2,1)S(1)} %bitcast.304, bf16[640,5120]{1,0:T(8,128)(2,1)} %param.31), kind=kOutput, calls=%fused_computation.59 | convolution fusion | flops 1679032320 | bytes 9502720 | tf_op jit(solution)/shard_map/dot_general | solution.py:120
  130.1 121.3 %while.39 = (s32[]{:T(128)}, bf16[256,256]{1,0:T(8,128)(2,1)S(1)}, bf16[256,256]{0,1:T(8,128)(2,1)S(1)}, f32[1,5,256,128]{3,2,1,0:T(8,128)S(1)}, s32[2]{0:T(128)...) while((s32[]{:T(128)}, bf16[256,256]{1,0:T(8,128)(2,1)S(1)}, ...), condition=%wide.region_9.11_spmd, body=%wide.region_8.10_spmd.sunk | while | flops 422940448 | bytes 10969655 | solution.py:185
  130.1 1.9 collective-permute-start.1
  134.1 0.6 fusion.110
  134.7 2.5 select_select_fusion.7
  137.3 4.2 %collective-permute-done.1 = bf16[256,256]{1,0:T(8,128)(2,1)S(1)} collective-permute-done((bf16[256,256]{1,0:T(8,128)(2,1)S(1)}, bf16[256,256]{1,0:T(8,128)(2,1)S(1)}, u32[]{:S(2)}, u32[]{:S(2)}) %collective-permute-start.1) | collective-permute-done | bytes 131104 | tf_op jit(solution)/shard_map/while/body/eval_jaxpr/ppermute | solution.py:18
  143.5 1.9 collective-permute-start.1
  147.5 0.6 fusion.110
  148.1 2.5 select_select_fusion.7
  150.7 4.3 %collective-permute-done.1 = bf16[256,256]{1,0:T(8,128)(2,1)S(1)} collective-permute-done((bf16[256,256]{1,0:T(8,128)(2,1)S(1)}, bf16[256,256]{1,0:T(8,128)(2,1)S(1)}, u32[]{:S(2)}, u32[]{:S(2)}) %collective-permute-start.1) | collective-permute-done | bytes 131104 | tf_op jit(solution)/shard_map/while/body/eval_jaxpr/ppermute | solution.py:18
  157.6 1.9 collective-permute-start.1
  159.5 4.0 %collective-permute-start.2 = (bf16[256,256]{0,1:T(8,128)(2,1)S(1)}, bf16[256,256]{0,1:T(8,128)(2,1)S(1)}, u32[]{:S(2)}, u32[]{:S(2)}) collective-permute-start(bf16[256,256]{0,1:T(8,128)(2,1)S(1)} %get-tuple-element.1145), channel_id=1, source_target_pairs={{0,4},{4,8},{8,12},{12,16},{16,20},{20,24},{24,28},{28,32},{32,36}... | collective-permute-start | bytes 393224 | tf_op jit(solution)/shard_map/while/body/eval_jaxpr/ppermute | solution.py:23
  166.1 2.5 select_select_fusion.7
  171.1 7.1 %collective-permute-start.1 = (bf16[256,256]{1,0:T(8,128)(2,1)S(1)}, bf16[256,256]{1,0:T(8,128)(2,1)S(1)}, u32[]{:S(2)}, u32[]{:S(2)}) collective-permute-start(bf16[256,256]{1,0:T(8,128)(2,1)S(1)} %get-tuple-element.1144), channel_id=1, source_target_pairs={{0,4},{4,8},{8,12},{12,16},{16,20},{20,24},{24,28},{28,32},{32,36}... | collective-permute-start | bytes 393224 | tf_op jit(solution)/shard_map/while/body/eval_jaxpr/ppermute | solution.py:18
  178.2 5.6 %collective-permute-start.2 = (bf16[256,256]{0,1:T(8,128)(2,1)S(1)}, bf16[256,256]{0,1:T(8,128)(2,1)S(1)}, u32[]{:S(2)}, u32[]{:S(2)}) collective-permute-start(bf16[256,256]{0,1:T(8,128)(2,1)S(1)} %get-tuple-element.1145), channel_id=1, source_target_pairs={{0,4},{4,8},{8,12},{12,16},{16,20},{20,24},{24,28},{28,32},{32,36}... | collective-permute-start | bytes 393224 | tf_op jit(solution)/shard_map/while/body/eval_jaxpr/ppermute | solution.py:23
  186.3 2.5 select_select_fusion.7
  191.0 1.9 collective-permute-start.1
  192.9 5.5 %collective-permute-start.2 = (bf16[256,256]{0,1:T(8,128)(2,1)S(1)}, bf16[256,256]{0,1:T(8,128)(2,1)S(1)}, u32[]{:S(2)}, u32[]{:S(2)}) collective-permute-start(bf16[256,256]{0,1:T(8,128)(2,1)S(1)} %get-tuple-element.1145), channel_id=1, source_target_pairs={{0,4},{4,8},{8,12},{12,16},{16,20},{20,24},{24,28},{28,32},{32,36}... | collective-permute-start | bytes 393224 | tf_op jit(solution)/shard_map/while/body/eval_jaxpr/ppermute | solution.py:23
  200.4 0.6 fusion.110
  201.0 2.5 select_select_fusion.7
  205.7 1.9 collective-permute-start.1
  207.6 5.6 %collective-permute-start.2 = (bf16[256,256]{0,1:T(8,128)(2,1)S(1)}, bf16[256,256]{0,1:T(8,128)(2,1)S(1)}, u32[]{:S(2)}, u32[]{:S(2)}) collective-permute-start(bf16[256,256]{0,1:T(8,128)(2,1)S(1)} %get-tuple-element.1145), channel_id=1, source_target_pairs={{0,4},{4,8},{8,12},{12,16},{16,20},{20,24},{24,28},{28,32},{32,36}... | collective-permute-start | bytes 393224 | tf_op jit(solution)/shard_map/while/body/eval_jaxpr/ppermute | solution.py:23
  215.7 2.5 select_select_fusion.7
  220.8 1.9 collective-permute-start.1
  222.7 5.7 %collective-permute-start.2 = (bf16[256,256]{0,1:T(8,128)(2,1)S(1)}, bf16[256,256]{0,1:T(8,128)(2,1)S(1)}, u32[]{:S(2)}, u32[]{:S(2)}) collective-permute-start(bf16[256,256]{0,1:T(8,128)(2,1)S(1)} %get-tuple-element.1145), channel_id=1, source_target_pairs={{0,4},{4,8},{8,12},{12,16},{16,20},{20,24},{24,28},{28,32},{32,36}... | collective-permute-start | bytes 393224 | tf_op jit(solution)/shard_map/while/body/eval_jaxpr/ppermute | solution.py:23
  231.0 2.5 select_select_fusion.7
  235.8 1.9 collective-permute-start.1
  237.7 6.5 %collective-permute-start.2 = (bf16[256,256]{0,1:T(8,128)(2,1)S(1)}, bf16[256,256]{0,1:T(8,128)(2,1)S(1)}, u32[]{:S(2)}, u32[]{:S(2)}) collective-permute-start(bf16[256,256]{0,1:T(8,128)(2,1)S(1)} %get-tuple-element.1145), channel_id=1, source_target_pairs={{0,4},{4,8},{8,12},{12,16},{16,20},{20,24},{24,28},{28,32},{32,36}... | collective-permute-start | bytes 393224 | tf_op jit(solution)/shard_map/while/body/eval_jaxpr/ppermute | solution.py:23
  246.7 2.5 select_select_fusion.7
  251.8 0.9 copy.52
  252.7 17.0 %collective-permute-done.3 = bf16[256,256]{1,0:T(8,128)(2,1)S(1)} collective-permute-done((bf16[256,256]{1,0:T(8,128)(2,1)S(1)}, bf16[256,256]{1,0:T(8,128)(2,1)S(1)}, u32[]{:S(2)}, u32[]{:S(2)}) %collective-permute-start.3) | collective-permute-done | bytes 131104 | tf_op jit(solution)/shard_map/ppermute | solution.py:23
  269.7 0.7 fusion.61
  (262 shorter events, 61.0 us)
Async XLA Ops:
  7.2 3.3 %copy-start.1 = (bf16[256,128]{1,0:T(8,128)(2,1)S(1)}, bf16[256,128]{1,0:T(8,128)(2,1)}, u32[]{:S(2)}) copy-start(bf16[256,128]{1,0:T(8,128)(2,1)} %param.29) | copy-start | bytes 196612
  7.2 108.4 %all-gather.2.cloned.1.call-start = ((), (), s32[]{:S(2)}) async-start(), calls=%async_computation.2 | async-start | bytes 3276800 | tf_op jit(solution)/shard_map/all_gather | solution.py:125
  7.9 262.4 %reduce-scatter.2.cloned.1.call-start = ((), (), s32[]{:S(2)}) async-start(), calls=%async_computation.1 | async-start | bytes 3276800 | tf_op jit(solution)/shard_map/reduce_scatter | solution.py:121
  12.2 0.8 copy-start
  12.7 0.9 copy-start.2
  13.6 11.6 %collective-permute-start = (bf16[256,256]{1,0:T(8,128)(2,1)S(1)}, bf16[256,256]{1,0:T(8,128)(2,1)S(1)}, u32[]{:S(2)}, u32[]{:S(2)}) collective-permute-start(bf16[256,256]{1,0:T(8,128)(2,1)S(1)} %get-tuple-element.1088), channel_id=1, source_target_pairs={{0,4},{4,8},{8,12},{12,16},{16,20},{20,24},{24,28},{28,32},{32,36}... | collective-permute-start | bytes 393224 | tf_op jit(solution)/shard_map/while/body/eval_jaxpr/ppermute | solution.py:18
  26.5 11.5 %collective-permute-start = (bf16[256,256]{1,0:T(8,128)(2,1)S(1)}, bf16[256,256]{1,0:T(8,128)(2,1)S(1)}, u32[]{:S(2)}, u32[]{:S(2)}) collective-permute-start(bf16[256,256]{1,0:T(8,128)(2,1)S(1)} %get-tuple-element.1088), channel_id=1, source_target_pairs={{0,4},{4,8},{8,12},{12,16},{16,20},{20,24},{24,28},{28,32},{32,36}... | collective-permute-start | bytes 393224 | tf_op jit(solution)/shard_map/while/body/eval_jaxpr/ppermute | solution.py:18
  39.3 11.5 %collective-permute-start = (bf16[256,256]{1,0:T(8,128)(2,1)S(1)}, bf16[256,256]{1,0:T(8,128)(2,1)S(1)}, u32[]{:S(2)}, u32[]{:S(2)}) collective-permute-start(bf16[256,256]{1,0:T(8,128)(2,1)S(1)} %get-tuple-element.1088), channel_id=1, source_target_pairs={{0,4},{4,8},{8,12},{12,16},{16,20},{20,24},{24,28},{28,32},{32,36}... | collective-permute-start | bytes 393224 | tf_op jit(solution)/shard_map/while/body/eval_jaxpr/ppermute | solution.py:18
  52.0 11.4 %collective-permute-start = (bf16[256,256]{1,0:T(8,128)(2,1)S(1)}, bf16[256,256]{1,0:T(8,128)(2,1)S(1)}, u32[]{:S(2)}, u32[]{:S(2)}) collective-permute-start(bf16[256,256]{1,0:T(8,128)(2,1)S(1)} %get-tuple-element.1088), channel_id=1, source_target_pairs={{0,4},{4,8},{8,12},{12,16},{16,20},{20,24},{24,28},{28,32},{32,36}... | collective-permute-start | bytes 393224 | tf_op jit(solution)/shard_map/while/body/eval_jaxpr/ppermute | solution.py:18
  64.7 11.4 %collective-permute-start = (bf16[256,256]{1,0:T(8,128)(2,1)S(1)}, bf16[256,256]{1,0:T(8,128)(2,1)S(1)}, u32[]{:S(2)}, u32[]{:S(2)}) collective-permute-start(bf16[256,256]{1,0:T(8,128)(2,1)S(1)} %get-tuple-element.1088), channel_id=1, source_target_pairs={{0,4},{4,8},{8,12},{12,16},{16,20},{20,24},{24,28},{28,32},{32,36}... | collective-permute-start | bytes 393224 | tf_op jit(solution)/shard_map/while/body/eval_jaxpr/ppermute | solution.py:18
  77.4 11.4 %collective-permute-start = (bf16[256,256]{1,0:T(8,128)(2,1)S(1)}, bf16[256,256]{1,0:T(8,128)(2,1)S(1)}, u32[]{:S(2)}, u32[]{:S(2)}) collective-permute-start(bf16[256,256]{1,0:T(8,128)(2,1)S(1)} %get-tuple-element.1088), channel_id=1, source_target_pairs={{0,4},{4,8},{8,12},{12,16},{16,20},{20,24},{24,28},{28,32},{32,36}... | collective-permute-start | bytes 393224 | tf_op jit(solution)/shard_map/while/body/eval_jaxpr/ppermute | solution.py:18
  90.0 11.4 %collective-permute-start = (bf16[256,256]{1,0:T(8,128)(2,1)S(1)}, bf16[256,256]{1,0:T(8,128)(2,1)S(1)}, u32[]{:S(2)}, u32[]{:S(2)}) collective-permute-start(bf16[256,256]{1,0:T(8,128)(2,1)S(1)} %get-tuple-element.1088), channel_id=1, source_target_pairs={{0,4},{4,8},{8,12},{12,16},{16,20},{20,24},{24,28},{28,32},{32,36}... | collective-permute-start | bytes 393224 | tf_op jit(solution)/shard_map/while/body/eval_jaxpr/ppermute | solution.py:18
  102.7 11.4 %collective-permute-start = (bf16[256,256]{1,0:T(8,128)(2,1)S(1)}, bf16[256,256]{1,0:T(8,128)(2,1)S(1)}, u32[]{:S(2)}, u32[]{:S(2)}) collective-permute-start(bf16[256,256]{1,0:T(8,128)(2,1)S(1)} %get-tuple-element.1088), channel_id=1, source_target_pairs={{0,4},{4,8},{8,12},{12,16},{16,20},{20,24},{24,28},{28,32},{32,36}... | collective-permute-start | bytes 393224 | tf_op jit(solution)/shard_map/while/body/eval_jaxpr/ppermute | solution.py:18
  130.1 11.4 %collective-permute-start.1 = (bf16[256,256]{1,0:T(8,128)(2,1)S(1)}, bf16[256,256]{1,0:T(8,128)(2,1)S(1)}, u32[]{:S(2)}, u32[]{:S(2)}) collective-permute-start(bf16[256,256]{1,0:T(8,128)(2,1)S(1)} %get-tuple-element.1144), channel_id=1, source_target_pairs={{0,4},{4,8},{8,12},{12,16},{16,20},{20,24},{24,28},{28,32},{32,36}... | collective-permute-start | bytes 393224 | tf_op jit(solution)/shard_map/while/body/eval_jaxpr/ppermute | solution.py:18
  132.0 11.4 %collective-permute-start.2 = (bf16[256,256]{0,1:T(8,128)(2,1)S(1)}, bf16[256,256]{0,1:T(8,128)(2,1)S(1)}, u32[]{:S(2)}, u32[]{:S(2)}) collective-permute-start(bf16[256,256]{0,1:T(8,128)(2,1)S(1)} %get-tuple-element.1145), channel_id=1, source_target_pairs={{0,4},{4,8},{8,12},{12,16},{16,20},{20,24},{24,28},{28,32},{32,36}... | collective-permute-start | bytes 393224 | tf_op jit(solution)/shard_map/while/body/eval_jaxpr/ppermute | solution.py:23
  143.5 11.5 %collective-permute-start.1 = (bf16[256,256]{1,0:T(8,128)(2,1)S(1)}, bf16[256,256]{1,0:T(8,128)(2,1)S(1)}, u32[]{:S(2)}, u32[]{:S(2)}) collective-permute-start(bf16[256,256]{1,0:T(8,128)(2,1)S(1)} %get-tuple-element.1144), channel_id=1, source_target_pairs={{0,4},{4,8},{8,12},{12,16},{16,20},{20,24},{24,28},{28,32},{32,36}... | collective-permute-start | bytes 393224 | tf_op jit(solution)/shard_map/while/body/eval_jaxpr/ppermute | solution.py:18
  145.4 12.1 %collective-permute-start.2 = (bf16[256,256]{0,1:T(8,128)(2,1)S(1)}, bf16[256,256]{0,1:T(8,128)(2,1)S(1)}, u32[]{:S(2)}, u32[]{:S(2)}) collective-permute-start(bf16[256,256]{0,1:T(8,128)(2,1)S(1)} %get-tuple-element.1145), channel_id=1, source_target_pairs={{0,4},{4,8},{8,12},{12,16},{16,20},{20,24},{24,28},{28,32},{32,36}... | collective-permute-start | bytes 393224 | tf_op jit(solution)/shard_map/while/body/eval_jaxpr/ppermute | solution.py:23
  157.6 11.5 %collective-permute-start.1 = (bf16[256,256]{1,0:T(8,128)(2,1)S(1)}, bf16[256,256]{1,0:T(8,128)(2,1)S(1)}, u32[]{:S(2)}, u32[]{:S(2)}) collective-permute-start(bf16[256,256]{1,0:T(8,128)(2,1)S(1)} %get-tuple-element.1144), channel_id=1, source_target_pairs={{0,4},{4,8},{8,12},{12,16},{16,20},{20,24},{24,28},{28,32},{32,36}... | collective-permute-start | bytes 393224 | tf_op jit(solution)/shard_map/while/body/eval_jaxpr/ppermute | solution.py:18
  159.5 11.5 %collective-permute-start.2 = (bf16[256,256]{0,1:T(8,128)(2,1)S(1)}, bf16[256,256]{0,1:T(8,128)(2,1)S(1)}, u32[]{:S(2)}, u32[]{:S(2)}) collective-permute-start(bf16[256,256]{0,1:T(8,128)(2,1)S(1)} %get-tuple-element.1145), channel_id=1, source_target_pairs={{0,4},{4,8},{8,12},{12,16},{16,20},{20,24},{24,28},{28,32},{32,36}... | collective-permute-start | bytes 393224 | tf_op jit(solution)/shard_map/while/body/eval_jaxpr/ppermute | solution.py:23
  171.1 17.8 %collective-permute-start.1 = (bf16[256,256]{1,0:T(8,128)(2,1)S(1)}, bf16[256,256]{1,0:T(8,128)(2,1)S(1)}, u32[]{:S(2)}, u32[]{:S(2)}) collective-permute-start(bf16[256,256]{1,0:T(8,128)(2,1)S(1)} %get-tuple-element.1144), channel_id=1, source_target_pairs={{0,4},{4,8},{8,12},{12,16},{16,20},{20,24},{24,28},{28,32},{32,36}... | collective-permute-start | bytes 393224 | tf_op jit(solution)/shard_map/while/body/eval_jaxpr/ppermute | solution.py:18
  178.2 12.8 %collective-permute-start.2 = (bf16[256,256]{0,1:T(8,128)(2,1)S(1)}, bf16[256,256]{0,1:T(8,128)(2,1)S(1)}, u32[]{:S(2)}, u32[]{:S(2)}) collective-permute-start(bf16[256,256]{0,1:T(8,128)(2,1)S(1)} %get-tuple-element.1145), channel_id=1, source_target_pairs={{0,4},{4,8},{8,12},{12,16},{16,20},{20,24},{24,28},{28,32},{32,36}... | collective-permute-start | bytes 393224 | tf_op jit(solution)/shard_map/while/body/eval_jaxpr/ppermute | solution.py:23
  191.0 12.6 %collective-permute-start.1 = (bf16[256,256]{1,0:T(8,128)(2,1)S(1)}, bf16[256,256]{1,0:T(8,128)(2,1)S(1)}, u32[]{:S(2)}, u32[]{:S(2)}) collective-permute-start(bf16[256,256]{1,0:T(8,128)(2,1)S(1)} %get-tuple-element.1144), channel_id=1, source_target_pairs={{0,4},{4,8},{8,12},{12,16},{16,20},{20,24},{24,28},{28,32},{32,36}... | collective-permute-start | bytes 393224 | tf_op jit(solution)/shard_map/while/body/eval_jaxpr/ppermute | solution.py:18
  192.9 12.7 %collective-permute-start.2 = (bf16[256,256]{0,1:T(8,128)(2,1)S(1)}, bf16[256,256]{0,1:T(8,128)(2,1)S(1)}, u32[]{:S(2)}, u32[]{:S(2)}) collective-permute-start(bf16[256,256]{0,1:T(8,128)(2,1)S(1)} %get-tuple-element.1145), channel_id=1, source_target_pairs={{0,4},{4,8},{8,12},{12,16},{16,20},{20,24},{24,28},{28,32},{32,36}... | collective-permute-start | bytes 393224 | tf_op jit(solution)/shard_map/while/body/eval_jaxpr/ppermute | solution.py:23
  205.7 12.7 %collective-permute-start.1 = (bf16[256,256]{1,0:T(8,128)(2,1)S(1)}, bf16[256,256]{1,0:T(8,128)(2,1)S(1)}, u32[]{:S(2)}, u32[]{:S(2)}) collective-permute-start(bf16[256,256]{1,0:T(8,128)(2,1)S(1)} %get-tuple-element.1144), channel_id=1, source_target_pairs={{0,4},{4,8},{8,12},{12,16},{16,20},{20,24},{24,28},{28,32},{32,36}... | collective-permute-start | bytes 393224 | tf_op jit(solution)/shard_map/while/body/eval_jaxpr/ppermute | solution.py:18
  207.6 13.2 %collective-permute-start.2 = (bf16[256,256]{0,1:T(8,128)(2,1)S(1)}, bf16[256,256]{0,1:T(8,128)(2,1)S(1)}, u32[]{:S(2)}, u32[]{:S(2)}) collective-permute-start(bf16[256,256]{0,1:T(8,128)(2,1)S(1)} %get-tuple-element.1145), channel_id=1, source_target_pairs={{0,4},{4,8},{8,12},{12,16},{16,20},{20,24},{24,28},{28,32},{32,36}... | collective-permute-start | bytes 393224 | tf_op jit(solution)/shard_map/while/body/eval_jaxpr/ppermute | solution.py:23
  220.8 12.8 %collective-permute-start.1 = (bf16[256,256]{1,0:T(8,128)(2,1)S(1)}, bf16[256,256]{1,0:T(8,128)(2,1)S(1)}, u32[]{:S(2)}, u32[]{:S(2)}) collective-permute-start(bf16[256,256]{1,0:T(8,128)(2,1)S(1)} %get-tuple-element.1144), channel_id=1, source_target_pairs={{0,4},{4,8},{8,12},{12,16},{16,20},{20,24},{24,28},{28,32},{32,36}... | collective-permute-start | bytes 393224 | tf_op jit(solution)/shard_map/while/body/eval_jaxpr/ppermute | solution.py:18
  222.7 13.0 %collective-permute-start.2 = (bf16[256,256]{0,1:T(8,128)(2,1)S(1)}, bf16[256,256]{0,1:T(8,128)(2,1)S(1)}, u32[]{:S(2)}, u32[]{:S(2)}) collective-permute-start(bf16[256,256]{0,1:T(8,128)(2,1)S(1)} %get-tuple-element.1145), channel_id=1, source_target_pairs={{0,4},{4,8},{8,12},{12,16},{16,20},{20,24},{24,28},{28,32},{32,36}... | collective-permute-start | bytes 393224 | tf_op jit(solution)/shard_map/while/body/eval_jaxpr/ppermute | solution.py:23
  235.8 13.6 %collective-permute-start.1 = (bf16[256,256]{1,0:T(8,128)(2,1)S(1)}, bf16[256,256]{1,0:T(8,128)(2,1)S(1)}, u32[]{:S(2)}, u32[]{:S(2)}) collective-permute-start(bf16[256,256]{1,0:T(8,128)(2,1)S(1)} %get-tuple-element.1144), channel_id=1, source_target_pairs={{0,4},{4,8},{8,12},{12,16},{16,20},{20,24},{24,28},{28,32},{32,36}... | collective-permute-start | bytes 393224 | tf_op jit(solution)/shard_map/while/body/eval_jaxpr/ppermute | solution.py:18
  237.7 13.7 %collective-permute-start.2 = (bf16[256,256]{0,1:T(8,128)(2,1)S(1)}, bf16[256,256]{0,1:T(8,128)(2,1)S(1)}, u32[]{:S(2)}, u32[]{:S(2)}) collective-permute-start(bf16[256,256]{0,1:T(8,128)(2,1)S(1)} %get-tuple-element.1145), channel_id=1, source_target_pairs={{0,4},{4,8},{8,12},{12,16},{16,20},{20,24},{24,28},{28,32},{32,36}... | collective-permute-start | bytes 393224 | tf_op jit(solution)/shard_map/while/body/eval_jaxpr/ppermute | solution.py:23
  251.5 18.2 %collective-permute-start.3 = (bf16[256,256]{1,0:T(8,128)(2,1)S(1)}, bf16[256,256]{1,0:T(8,128)(2,1)S(1)}, u32[]{:S(2)}, u32[]{:S(2)}) collective-permute-start(bf16[256,256]{1,0:T(8,128)(2,1)S(1)} %copy.51), channel_id=1, source_target_pairs={{0,224},{4,228},{8,232},{12,236},{16,240},{20,244},{24,248},{28,25... | collective-permute-start | bytes 393224 | tf_op jit(solution)/shard_map/ppermute | solution.py:23
Sparse Core Ops, SparseCore 0:
  9.8 43.0 all-gather.1
  130.2 55.0 reduce-scatter.1
where the time goes:
time: 279 us; the launch traced here: 277 us
  starting transfers between devices  70.6 us (25%)
  waiting for transfers between devices  60.8 us (22%)
  other arithmetic  46.1 us (17%)
  matrix products  38 us (14%)
  local copies, waits for them, and re-layouts  34.9 us (13%)
  between operations  14.3 us (5%)
  loops' own time  12.4 us (4%)
    ppermute x16, waiting for transfers between devices, from_behind(): return lax.ppermute(array, axis, pairs)  42 us
    select_n x17, other arithmetic, doc_span(): return jnp.repeat(blocks, BLK, total_repeat_length=count)  40.9 us
    ppermute x16, starting transfers between devices, from_behind(): return lax.ppermute(array, axis, pairs)  37.4 us
    ppermute x9, starting transfers between devices, from_behind_2(): lax.ppermute(array, axis, [(i, (i + by) % devices) for i in range(devices)])  33.1 us
    gather x33, local copies, waits for them, and re-layouts, doc_span(): return jnp.repeat(blocks, BLK, total_repeat_length=count)  19.4 us
    ppermute x9, waiting for transfers between devices, from_behind_2(): lax.ppermute(array, axis, [(i, (i + by) % devices) for i in range(devices)])  18.1 us
    dynamic_slice x16, local copies, waits for them, and re-layouts, on_device(): lax.scan(forward_step, (key_value, state), steps_ahead)  9.38 us
    dot_general x1, matrix products, on_device(): partial_out = jnp.dot(attn, out_weight, preferred_element_type=jnp.float32)  6.62 us
  transfers between devices with their start and end apart: 27, of which 15 were waited for; matrix products, arithmetic and copies ran while one was open for 38% of the time, Pallas kernels for 0%

commit v1 on v0

v1 whole, which is shorter than its diff:
```python
import functools
import math

import jax
import jax.numpy as jnp
from jax import lax
from jax.experimental import pallas as pl
from jax.experimental.pallas import tpu as pltpu
from jax.sharding import PartitionSpec as P

HEAD = 128
BLK = 128
GROUP = 4
SLOTS = 2 * GROUP + 1
NEG = -1e30
F32 = jnp.float32
BF16 = jnp.bfloat16
MESH = pl.DeviceIdType.MESH


def dot(a, b):
    return lax.dot_general(a, b, (((1,), (0,)), ((), ())), preferred_element_type=F32)


def dot_t(a, b):
    return lax.dot_general(a, b, (((1,), (1,)), ((), ())), preferred_element_type=F32)


def kernel(
    n_ctx,
    heads,
    rows,
    chunks,
    doc,
    q_in,
    k_in,
    v_in,
    w_in,
    c_in,
    mixed,
    gq,
    gk,
    gv,
    qb,
    kv,
    wb,
    cb,
    qt,
    pb,
    mb,
    mrun,
    lrun,
    acc,
    attn_t,
    attn,
    dot_b,
    do_b,
    delta,
    dqt,
    gkv,
    g3,
    rx,
    rz,
    pp,
    pr,
    pc,
    xc,
    xr,
    po,
    q_sem,
    o_sem,
    w_sem,
    c_sem,
    ks,
    kr,
    cs,
    cr,
    gs,
    gr,
    zs,
    zr,
    ps,
    prs,
    xs,
    xrs,
):
    i = lax.axis_index("ctx")
    t = lax.axis_index("tp")
    x = lax.rem(i, GROUP)
    g0 = i - x
    partner = t + 1 - 2 * lax.rem(t, 2)
    cross = lax.rem(t + 2, 4)
    diag = lax.rem(partner + 2, 4)
    scale = 1.0 / math.sqrt(HEAD)
    c2 = scale * math.log2(math.e)

    def ctx_at(by):
        return lax.rem(i + by + n_ctx, n_ctx)

    def peer(e):
        return g0 + lax.rem(x + e + GROUP, GROUP)

    own_k = pltpu.make_async_copy(k_in, kv.at[0, 0], o_sem.at[0])
    own_v = pltpu.make_async_copy(v_in, kv.at[0, 1], o_sem.at[1])
    own_k.start()
    own_v.start()
    q_copy = pltpu.make_async_copy(q_in, qb, q_sem)
    q_copy.start()
    own_c = pltpu.make_async_copy(c_in, cb.at[t], c_sem)
    own_c.start()
    width = chunks * 256

    def w_copy(s):
        return pltpu.make_async_copy(
            w_in.at[:, pl.ds(pl.multiple_of(s * width, 256), width)], wb.at[s], w_sem.at[s]
        )

    for s in range(4):
        w_copy(s).start()

    barrier = pltpu.get_barrier_semaphore()
    for by in (4, -4, 8, -8):
        pl.semaphore_signal(barrier, inc=1, device_id=(ctx_at(by), t), device_id_type=MESH)
    for e in (1, 2, 3):
        pl.semaphore_signal(barrier, inc=1, device_id=(peer(e), t), device_id_type=MESH)
    for other in (partner, cross):
        pl.semaphore_signal(barrier, inc=1, device_id=(i, other), device_id_type=MESH)
    pl.semaphore_wait(barrier, 9)

    def send(src, dst, s_sem, r_sem, ctx, tp):
        return pltpu.make_async_remote_copy(
            src_ref=src,
            dst_ref=dst,
            send_sem=s_sem,
            recv_sem=r_sem,
            device_id=(ctx, tp),
            device_id_type=MESH,
        )

    def far(slot):
        return send(kv.at[0], kv.at[slot], ks.at[slot], kr.at[slot], ctx_at(slot), t)

    def near(src, slot, e):
        return send(kv.at[src], kv.at[slot], ks.at[slot], kr.at[slot], peer(e), t)

    def cot_send(c, to, k):
        cols = pl.ds(c * 256, 256)
        return send(c_in.at[:, cols], cb.at[t, :, cols], cs.at[k, c], cr.at[t, c], i, to)

    def cot_pass(c):
        cols = pl.ds(c * 256, 256)
        block = cb.at[cross, :, cols]
        return send(block, block, cs.at[2, c], cr.at[cross, c], i, partner)

    def cot_wait(s, c):
        cols = pl.ds(c * 256, 256)
        block = cb.at[s, :, cols]
        send(block, block, cs.at[0, c], cr.at[s, c], i, partner).wait_recv()

    own_k.wait()
    own_v.wait()
    far(4).start()
    far(8).start()
    for e in (2, 1, 3):

        @pl.when(x + e < GROUP)
        def _():
            near(0, e, e).start()

    for c in range(chunks):
        cot_send(c, cross, 0).start()
    for c in range(chunks):
        cot_send(c, partner, 1).start()

    q_copy.wait()
    for h in range(heads):
        qt[h] = qb[:, h * HEAD : (h + 1) * HEAD].T

    lane = lax.broadcasted_iota(jnp.int32, (1, rows), 1)
    q_doc = jnp.where(lane < BLK, doc[2 * i], doc[2 * i + 1])

    def first_slot():
        k_blk = kv[0, 0]
        v_t = kv[0, 1].T
        key = lax.broadcasted_iota(jnp.int32, (rows, rows), 0)
        query = lax.broadcasted_iota(jnp.int32, (rows, rows), 1)
        k_doc = jnp.where(key < BLK, doc[2 * i], doc[2 * i + 1])
        allowed = (key <= query) & (k_doc == q_doc)
        for h in range(heads):
            s = jnp.where(allowed, dot(k_blk, qt[h]) * c2, NEG)
            m = jnp.max(s, axis=0, keepdims=True)
            p = jnp.exp2(s - m)
            lrun[h] = jnp.sum(p, axis=0, keepdims=True)
            p = p.astype(BF16)
            pb[0, h] = p
            mrun[h] = m
            mb[0, h] = m
            acc[h] = dot(v_t, p)

    def fwd_slot(d):
        src = ctx_at(-d)
        k_blk = kv[d, 0]
        v_t = kv[d, 1].T
        b0 = jnp.where(q_doc == doc[2 * src], 0.0, NEG)
        b1 = jnp.where(q_doc == doc[2 * src + 1], 0.0, NEG)
        for h in range(heads):
            s = dot(k_blk, qt[h]) * c2
            s0, s1 = s[:BLK], s[BLK:]
            m_old = mrun[h]
            m = jnp.maximum(
                m_old,
                jnp.maximum(
                    jnp.max(s0, axis=0, keepdims=True) + b0,
                    jnp.max(s1, axis=0, keepdims=True) + b1,
                ),
            )
            alpha = jnp.exp2(m_old - m)
            p0 = jnp.exp2(s0 - (m - b0))
            p1 = jnp.exp2(s1 - (m - b1))
            lrun[h] = (
                lrun[h] * alpha
                + jnp.sum(p0, axis=0, keepdims=True)
                + jnp.sum(p1, axis=0, keepdims=True)
            )
            p = jnp.concatenate([p0, p1], axis=0).astype(BF16)
            pb[d, h] = p
            mrun[h] = m
            mb[d, h] = m
            acc[h] = acc[h] * alpha + dot(v_t, p)

    first_slot()
    far(4).wait_recv()
    for e in (2, 1, 3):

        @pl.when(x + e < GROUP)
        def _():
            near(4, e + 4, e).start()

        @pl.when(x + e >= GROUP)
        def _():
            near(4, e, e).start()

    far(8).wait_recv()
    for e in (2, 1, 3):

        @pl.when(x + e >= GROUP)
        def _():
            near(8, e + 4, e).start()

    def fwd_step(k, carry):
        d = jnp.where(k < 2, 4 * (k + 1), jnp.where(k < 5, k - 1, k))
        d = jnp.where(k == 3, 3, jnp.where(k == 4, 2, jnp.where(k == 6, 7, jnp.where(k == 7, 6, d))))

        @pl.when(k >= 2)
        def _():
            near(0, d, 1).wait_recv()

        fwd_slot(d)
        return carry

    lax.fori_loop(0, SLOTS - 1, fwd_step, 0)

    for h in range(heads):
        a = (acc[h] / lrun[h]).astype(BF16)
        attn_t[h] = a
        attn[:, h * HEAD : (h + 1) * HEAD] = a.T

    def part(s, c):
        cols = pl.ds(pl.multiple_of(c * 256, 256), 256)
        return dot(attn[...], wb[s, :, cols])

    def to_partner(k, c):
        return send(pp.at[k, c], pr.at[k, c], ps.at[k, c], prs.at[k, c], i, partner)

    def to_cross(c):
        return send(xc.at[c], xr.at[c], xs.at[c], xrs.at[c], i, cross)

    for s in range(4):
        w_copy(s).wait()

    def diag_step(c, carry):
        pp[0, c] = part(diag, c).astype(BF16)
        to_partner(0, c).start()
        return carry

    lax.fori_loop(0, chunks, diag_step, 0)

    def cross_step(c, carry):
        mine = part(cross, c)
        to_partner(0, c).wait_recv()
        xc[c] = (mine + pr[0, c].astype(F32)).astype(BF16)
        to_cross(c).start()
        return carry

    lax.fori_loop(0, chunks, cross_step, 0)

    def partner_step(c, carry):
        pp[1, c] = part(partner, c).astype(BF16)
        to_partner(1, c).start()
        po[c] = part(t, c)
        return carry

    lax.fori_loop(0, chunks, partner_step, 0)

    for c in range(chunks):
        cot_wait(cross, c)
        cot_pass(c).start()
    own_c.wait()
    grad = dot_t(wb[t], cb[t])
    for c in range(chunks):
        cot_wait(partner, c)
    grad = grad + dot_t(wb[partner], cb[partner])
    grad = grad + dot_t(wb[cross], cb[cross])
    for c in range(chunks):
        cot_wait(diag, c)
    grad = grad + dot_t(wb[diag], cb[diag])
    for h in range(heads):
        do_t = grad[h * HEAD : (h + 1) * HEAD].astype(BF16)
        dot_b[h] = do_t
        do_b[h] = do_t.T
        delta[h] = jnp.sum(do_t.astype(F32) * attn_t[h].astype(F32), axis=0, keepdims=True)
        dqt[h] = jnp.zeros((HEAD, rows), F32)
        lrun[h] = 1.0 / lrun[h]

    def bwd_slot(d):
        k_t = kv[d, 0].T
        v_blk = kv[d, 1]
        dk = jnp.zeros((rows, HEAD), F32)
        dv = jnp.zeros((rows, HEAD), F32)
        for h in range(heads):
            f = jnp.exp2(mb[d, h] - mrun[h]) * lrun[h]
            p = pb[d, h].astype(F32) * f
            dv = dv + dot(p.astype(BF16), do_b[h])
            ds = (p * (dot(v_blk, dot_b[h]) - delta[h])).astype(BF16)
            dk = dk + dot(ds, qb[:, h * HEAD : (h + 1) * HEAD])
            dqt[h] = dqt[h] + dot(k_t, ds)
        return dk * scale, dv

    def grad_near(e, j):
        return send(
            gkv.at[e + 4 * j], rx.at[e - 1, j], gs.at[e - 1, j], gr.at[e - 1, j], peer(-e), t
        )

    def bwd_step(k, carry):
        e = jnp.where(k < 2, 2, jnp.where(k < 4, 1, 3))
        j = lax.rem(k, 2)
        d = e + 4 * j
        dk, dv = bwd_slot(d)
        gkv[d, 0] = dk.astype(BF16)
        gkv[d, 1] = dv.astype(BF16)
        grad_near(e, j).start()
        return carry

    lax.fori_loop(0, 6, bwd_step, 0)

    def bwd_own(k, carry):
        dk, dv = bwd_slot(8 - 4 * k)
        g3[2 - k, 0] = dk
        g3[2 - k, 1] = dv
        return carry

    lax.fori_loop(0, 3, bwd_own, 0)

    for e in (2, 1, 3):
        base = lax.div(x + e, GROUP)
        for j in range(2):
            grad_near(e, j).wait_recv()
            g3[base + j] = g3[base + j] + rx[e - 1, j].astype(F32)

    def grad_far(k):
        return send(gkv.at[4 * k + 4], rz.at[k], zs.at[k], zr.at[k], ctx_at(-4 * k - 4), t)

    for k in range(2):
        gkv[4 * k + 4] = g3[k + 1].astype(BF16)
        grad_far(k).start()

    for h in range(heads):
        gq[:, h * HEAD : (h + 1) * HEAD] = (dqt[h].T * scale).astype(BF16)
    for c in range(chunks):
        to_partner(1, c).wait_recv()
        to_cross(c).wait_recv()
        mixed[:, c * 256 : (c + 1) * 256] = (
            po[c] + pr[1, c].astype(F32) + xr[c].astype(F32)
        ).astype(BF16)
    for k in range(2):
        grad_far(k).wait_recv()
    total = g3[0] + rz[0].astype(F32) + rz[1].astype(F32)
    gk[...] = total[0].astype(BF16)
    gv[...] = total[1].astype(BF16)

    for slot in (4, 8):
        far(slot).wait_send()
    for e in (1, 2, 3):
        near(0, e, e).wait_send()
        near(0, e + 4, e).wait_send()
        for j in range(2):
            grad_near(e, j).wait_send()
    for k in range(2):
        grad_far(k).wait_send()
    for c in range(chunks):
        cot_send(c, cross, 0).wait_send()
        cot_send(c, partner, 1).wait_send()
        cot_pass(c).wait_send()
        to_partner(0, c).wait_send()
        to_partner(1, c).wait_send()
        to_cross(c).wait_send()


def on_device(queries, keys, values, out_weight, cotangent, doc_ids):
    n_ctx = lax.axis_size("ctx")
    rows = queries.shape[0]
    heads = queries.shape[1] // HEAD
    chunks = cotangent.shape[1] // 256
    any_space = pl.BlockSpec(memory_space=pl.ANY)
    vmem = pl.BlockSpec(memory_space=pltpu.VMEM)
    dma = pltpu.SemaphoreType.DMA
    return pl.pallas_call(
        functools.partial(kernel, n_ctx, heads, rows, chunks),
        out_shape=(
            jax.ShapeDtypeStruct(cotangent.shape, BF16),
            jax.ShapeDtypeStruct(queries.shape, BF16),
            jax.ShapeDtypeStruct(keys.shape, BF16),
            jax.ShapeDtypeStruct(values.shape, BF16),
        ),
        in_specs=[pl.BlockSpec(memory_space=pltpu.SMEM)] + [any_space] * 5,
        out_specs=(vmem,) * 4,
        scratch_shapes=[
            pltpu.VMEM((rows, heads * HEAD), BF16),
            pltpu.VMEM((SLOTS, 2, rows, HEAD), BF16),
            pltpu.VMEM((4, heads * HEAD, chunks * 256), BF16),
            pltpu.VMEM((4, rows, chunks * 256), BF16),
            pltpu.VMEM((heads, HEAD, rows), BF16),
            pltpu.VMEM((SLOTS, heads, rows, rows), BF16),
            pltpu.VMEM((SLOTS, heads, 1, rows), F32),
            pltpu.VMEM((heads, 1, rows), F32),
            pltpu.VMEM((heads, 1, rows), F32),
            pltpu.VMEM((heads, HEAD, rows), F32),
            pltpu.VMEM((heads, HEAD, rows), BF16),
            pltpu.VMEM((rows, heads * HEAD), BF16),
            pltpu.VMEM((heads, HEAD, rows), BF16),
            pltpu.VMEM((heads, rows, HEAD), BF16),
            pltpu.VMEM((heads, 1, rows), F32),
            pltpu.VMEM((heads, HEAD, rows), F32),
            pltpu.VMEM((SLOTS, 2, rows, HEAD), BF16),
            pltpu.VMEM((3, 2, rows, HEAD), F32),
            pltpu.VMEM((3, 2, 2, rows, HEAD), BF16),
            pltpu.VMEM((2, 2, rows, HEAD), BF16),
            pltpu.VMEM((2, chunks, rows, 256), BF16),
            pltpu.VMEM((2, chunks, rows, 256), BF16),
            pltpu.VMEM((1, 8, 128), F32),
            pltpu.VMEM((chunks, rows, 256), BF16),
            pltpu.VMEM((chunks, rows, 256), BF16),
            pltpu.VMEM((chunks, rows, 256), F32),
            dma,
            dma((2,)),
            dma((4,)),
            dma,
            dma((SLOTS,)),
            dma((SLOTS,)),
            dma((3, chunks)),
            dma((4, chunks)),
            dma((3, 2)),
            dma((3, 2)),
            dma((2,)),
            dma((2,)),
            dma((2, chunks)),
            dma((2, chunks)),
            dma((chunks,)),
            dma((chunks,)),
        ],
        compiler_params=pltpu.CompilerParams(
            collective_id=0, has_side_effects=True, vmem_limit_bytes=60 * 1024 * 1024
        ),
    )(doc_ids, queries, keys, values, out_weight, cotangent)


def solution(mesh):
    return jax.shard_map(
        on_device,
        mesh=mesh,
        in_specs=(
            P("ctx", "tp"),
            P("ctx", "tp"),
            P("ctx", "tp"),
            P("tp", None),
            P("ctx", "tp"),
            P(),
        ),
        out_specs=(P("ctx", "tp"), P("ctx", "tp"), P("ctx", "tp"), P("ctx", "tp")),
        check_vma=False,
    )
```

time: 279 us -> 76.5 us (0.27)
  the two profiles are of different devices: /device:TPU:96 before, /device:TPU:4 now
where the time goes in v1:
time: 76.5 us; the launch traced here: 76.2 us
  Pallas kernels  69 us (90%)
  local copies, waits for them, and re-layouts  6.63 us (9%)
    pallas_call x1, Pallas kernels, on_device(): pl.pallas_call(functools.partial(kernel, n_ctx, heads, rows, chunks), out...  69 us
    unnamed x4, local copies, waits for them, and re-layouts  6.63 us

profile of v1, /device:TPU:4, one launch (start us, length us, event | category | flops | bytes accessed | tf_op | source)
XLA Modules:
  0.0 76.2 jit_solution(14888039001254646280)
XLA Ops:
  0.6 69.0 %shard_map.93 = (bf16[256,1280]{1,0:T(8,128)(2,1)}, bf16[256,640]{1,0:T(8,128)(2,1)}, bf16[256,128]{1,0:T(8,128)(2,1)}, bf16[256,128]{1,0:T(8,128)(2,1)}) custom-call(s32[128]{0:T(128)} %doc.1, bf16[256,640]{1,0:T(8,128)(2,1)} %q_in.1, bf16[256,128]{1,0:T(8,128)(2,1)} %k_in.1, bf16[256,128]{1,0:T(8,128)(2,1)} %v_in.1, bf16[640,5120]{1,0:T(8,128)(2,1)} %w_in.1, ...), custom_call_target="tpu_custom_call" | custom-call | tf_op jit(solution)/shard_map/pallas_call | solution.py:417
  69.6 2.0 %copy.14 = bf16[256,1280]{1,0:T(8,128)(2,1)} copy(bf16[256,1280]{1,0:T(8,128)(2,1)} %get-tuple-element.8) | data formatting | bytes 1310720
  71.6 1.7 %copy.15 = bf16[256,640]{1,0:T(8,128)(2,1)} copy(bf16[256,640]{1,0:T(8,128)(2,1)} %get-tuple-element.9) | data formatting | bytes 655360
  73.3 1.5 %copy.16 = bf16[256,128]{1,0:T(8,128)(2,1)} copy(bf16[256,128]{1,0:T(8,128)(2,1)} %get-tuple-element.10) | data formatting | bytes 131072
  74.8 1.5 %copy.17 = bf16[256,128]{1,0:T(8,128)(2,1)} copy(bf16[256,128]{1,0:T(8,128)(2,1)} %get-tuple-element.11) | data formatting | bytes 131072

commit v2 on v1

v2 whole, which is shorter than its diff:
```python
import contextlib
import functools
import math

import jax
import jax.numpy as jnp
from jax import lax
from jax.experimental import pallas as pl
from jax.experimental.pallas import tpu as pltpu
from jax.sharding import PartitionSpec as P

HEAD = 128
BLK = 128
GROUP = 4
SLOTS = 2 * GROUP + 1
NEG = -1e30
F32 = jnp.float32
BF16 = jnp.bfloat16
MESH = pl.DeviceIdType.MESH


def dot(a, b):
    return lax.dot_general(a, b, (((1,), (0,)), ((), ())), preferred_element_type=F32)


def dot_t(a, b):
    return lax.dot_general(a, b, (((1,), (1,)), ((), ())), preferred_element_type=F32)


def scope(name):
    return contextlib.nullcontext()


def kernel(
    n_ctx,
    heads,
    rows,
    chunks,
    doc_in,
    q_in,
    k_in,
    v_in,
    w_in,
    c_in,
    mixed,
    gq,
    gk,
    gv,
    doc,
    qb,
    qs,
    kv,
    wb,
    cb,
    qt,
    sb,
    pb,
    mg,
    m8,
    mrun,
    l8,
    linv,
    acc,
    attn_t,
    attn,
    gt,
    dot_b,
    do_b,
    delta,
    ktb,
    gkv,
    g3,
    relay,
    rx,
    rz,
    pp,
    pr,
    xc,
    xr,
    po,
    d_sem,
    q_sem,
    o_sem,
    w_sem,
    c_sem,
    ks,
    kr,
    cs,
    cr,
    rs,
    rr,
    gs,
    gr,
    zs,
    zr,
    ps,
    prs,
    xs,
    xrs,
):
    i = lax.axis_index("ctx")
    t = lax.axis_index("tp")
    x = lax.rem(i, GROUP)
    g0 = i - x
    partner = t + 1 - 2 * lax.rem(t, 2)
    cross = lax.rem(t + 2, 4)
    diag = lax.rem(partner + 2, 4)
    scale = 1.0 / math.sqrt(HEAD)
    c2 = scale * math.log2(math.e)
    last = lax.div(x, GROUP - 1)
    first = lax.div(GROUP - 1 - x, GROUP - 1)

    def ctx_at(by):
        return lax.rem(i + by + n_ctx, n_ctx)

    def peer(e):
        return g0 + lax.rem(x + e + GROUP, GROUP)

    own_k = pltpu.make_async_copy(k_in, kv.at[0, 0], o_sem.at[0])
    own_v = pltpu.make_async_copy(v_in, kv.at[0, 1], o_sem.at[1])
    own_k.start()
    own_v.start()
    doc_copy = pltpu.make_async_copy(doc_in, doc, d_sem)
    doc_copy.start()
    q_copy = pltpu.make_async_copy(q_in, qb, q_sem)
    q_copy.start()
    own_c = pltpu.make_async_copy(c_in, cb.at[t], c_sem)
    own_c.start()
    width = chunks * 256

    def w_copy(s):
        return pltpu.make_async_copy(
            w_in.at[:, pl.ds(pl.multiple_of(s * width, 256), width)], wb.at[s], w_sem.at[s]
        )

    for s in (t, partner, diag, cross):
        w_copy(s).start()

    barrier = pltpu.get_barrier_semaphore()
    for by in (4, -4, 8, -8):
        pl.semaphore_signal(barrier, inc=1, device_id=(ctx_at(by), t), device_id_type=MESH)
    for e in (1, 3):
        pl.semaphore_signal(barrier, inc=1, device_id=(peer(e), t), device_id_type=MESH)
    for other in (partner, cross):
        pl.semaphore_signal(barrier, inc=1, device_id=(i, other), device_id_type=MESH)
    with scope("barrier"):
        pl.semaphore_wait(barrier, 8)

    def send(src, dst, s_sem, r_sem, ctx, tp):
        return pltpu.make_async_remote_copy(
            src_ref=src,
            dst_ref=dst,
            send_sem=s_sem,
            recv_sem=r_sem,
            device_id=(ctx, tp),
            device_id_type=MESH,
        )

    def far(place):
        return send(kv.at[0], kv.at[place], ks.at[place], kr.at[place], ctx_at(4 * place), t)

    def near(src, place, e):
        return send(kv.at[src], kv.at[place], ks.at[place], kr.at[place], peer(e), t)

    def arrived(place):
        near(0, place, 1).wait_recv()

    def cot_send(c, to, k):
        cols = pl.ds(c * 256, 256)
        return send(c_in.at[:, cols], cb.at[t, :, cols], cs.at[k, c], cr.at[t, c], i, to)

    def cot_pass(c):
        cols = pl.ds(c * 256, 256)
        block = cb.at[cross, :, cols]
        return send(block, block, cs.at[2, c], cr.at[cross, c], i, partner)

    def cot_wait(s, c):
        cols = pl.ds(c * 256, 256)
        block = cb.at[s, :, cols]
        send(block, block, cs.at[0, c], cr.at[s, c], i, partner).wait_recv()

    own_k.wait()
    own_v.wait()
    far(1).start()
    far(2).start()
    for e in (1, 3):

        @pl.when(x + e < GROUP)
        def _():
            near(0, 2 + e, e).start()

    for c in range(chunks):
        cot_send(c, partner, 1).start()

    q_copy.wait()
    doc_copy.wait()
    for h in range(heads):
        q_head = qb[:, h * HEAD : (h + 1) * HEAD]
        qs[h] = q_head
        qt[h] = q_head.T

    lane = lax.broadcasted_iota(jnp.int32, (1, rows), 1)
    q_doc = jnp.where(lane < BLK, doc[2 * i], doc[2 * i + 1])

    def bias(d):
        src = ctx_at(-d)
        return [jnp.where(q_doc == doc[2 * src + b], 0.0, NEG) for b in range(2)]

    def scores(k, place, d):
        k_blk = kv[place, 0]
        if d is None:
            key = lax.broadcasted_iota(jnp.int32, (rows, rows), 0)
            query = lax.broadcasted_iota(jnp.int32, (rows, rows), 1)
            k_doc = jnp.where(key < BLK, doc[2 * i], doc[2 * i + 1])
            allowed = (key <= query) & (k_doc == q_doc)
        else:
            b0, b1 = bias(d)
        for h in range(heads):
            s = dot(k_blk, qt[h])
            if d is None:
                s = jnp.where(allowed, s, NEG)
            sb[k, h] = s
            top = jnp.max(s.reshape(2, BLK // 8, 8, rows), axis=1) * c2
            if d is None:
                top = jnp.maximum(top[0], top[1])
            else:
                top = jnp.maximum(top[0] + b0, top[1] + b1)
            m8[h] = top if k == 0 else jnp.maximum(m8[h], top)

    def weigh(group, entries):
        tops = []
        alphas = []
        for h in range(heads):
            m = jnp.max(m8[h], axis=0, keepdims=True)
            if group > 0:
                m = jnp.maximum(m, mrun[h])
                alphas.append(jnp.exp2(mrun[h] - m))
            mrun[h] = m
            mg[group, h] = m
            tops.append(m)
        v_t = jnp.concatenate([kv[place, 1].T for place, _ in entries], axis=1)
        shifts = [None if d is None else bias(d) for _, d in entries]
        for h in range(heads):
            blocks = []
            total = None
            for k, (place, d) in enumerate(entries):
                s = sb[k, h] * c2
                if d is None:
                    p = jnp.exp2(s - tops[h])
                else:
                    b0, b1 = shifts[k]
                    p = jnp.concatenate(
                        [jnp.exp2(s[:BLK] - (tops[h] - b0)), jnp.exp2(s[BLK:] - (tops[h] - b1))],
                        axis=0,
                    )
                part_sum = jnp.sum(p.reshape(rows // 8, 8, rows), axis=0)
                total = part_sum if total is None else total + part_sum
                p = p.astype(BF16)
                pb[place, h] = p
                blocks.append(p)
            out = dot(v_t, jnp.concatenate(blocks, axis=0))
            if group > 0:
                total = total + l8[h] * alphas[h]
                out = out + acc[h] * alphas[h]
            l8[h] = total
            acc[h] = out

    with scope("slot0"):
        scores(0, 0, None)
    for c in range(chunks):
        cot_send(c, cross, 0).start()
    with scope("grad0"):
        w_copy(t).wait()
        own_c.wait()
        gt[...] = dot_t(wb[t], cb[t])
    with scope("wait4"):
        far(1).wait_recv()
    for e in (1, 3):

        @pl.when(x + e < GROUP)
        def _():
            near(1, 3 + e, e).start()

        @pl.when(x + e >= GROUP)
        def _():
            near(1, 2 + e, e).start()

    with scope("wait8"):
        far(2).wait_recv()
    for e in (1, 3):

        @pl.when(x + e >= GROUP)
        def _():
            near(2, 3 + e, e).start()

    with scope("groupA"):
        scores(1, 1, 4)
        scores(2, 2, 8)
        weigh(0, [(0, None), (1, 4), (2, 8)])

    up, down = 3 + last, 6 - first
    with scope("waitup"):
        arrived(up)
    near(up, 7, 1).start()
    with scope("waitdown"):
        arrived(down)
    near(down, 8, -1).start()
    with scope("grad1"):
        w_copy(partner).wait()
        for c in range(chunks):
            cot_wait(partner, c)
        gt[...] += dot_t(wb[partner], cb[partner])
    rest_up, rest_down = 4 - last, 5 + first
    group_b = [
        (up, 1 + 4 * last),
        (down, 7 - 4 * first),
        (rest_up, 5 - 4 * last),
        (rest_down, 3 + 4 * first),
    ]
    for k, (place, d) in enumerate(group_b):
        if k >= 2:
            with scope("waitb"):
                arrived(place)
        with scope("scoreb"):
            scores(k, place, d)
    with scope("groupB"):
        weigh(1, group_b)
    group_c = [(7, 2), (8, 6)]
    for k, (place, d) in enumerate(group_c):
        with scope("waitc"):
            arrived(place)
        scores(k, place, d)
    with scope("groupC"):
        weigh(2, group_c)

        for h in range(heads):
            inv = 1.0 / jnp.sum(l8[h], axis=0, keepdims=True)
            linv[h] = inv
            a = (acc[h] * inv).astype(BF16)
            attn_t[h] = a
            attn[:, h * HEAD : (h + 1) * HEAD] = a.T

    def part(s, c):
        return dot(attn[...], wb[s, :, c * 256 : (c + 1) * 256])

    def to_partner(k, c):
        return send(pp.at[k, c], pr.at[k, c], ps.at[k, c], prs.at[k, c], i, partner)

    def to_cross(c):
        return send(xc.at[c], xr.at[c], xs.at[c], xrs.at[c], i, cross)

    with scope("diag"):
        w_copy(diag).wait()
        for c in range(chunks):
            pp[0, c] = part(diag, c).astype(BF16)
            to_partner(0, c).start()
    with scope("cross"):
        w_copy(cross).wait()
        for c in range(chunks):
            po[c] = part(cross, c)
    with scope("rs1"):
        for c in range(chunks):
            to_partner(0, c).wait_recv()
            xc[c] = (po[c] + pr[0, c].astype(F32)).astype(BF16)
            to_cross(c).start()

    with scope("cotx"):
        for c in range(chunks):
            cot_wait(cross, c)
            cot_pass(c).start()
    with scope("grad2"):
        gt[...] += dot_t(wb[cross], cb[cross])
    with scope("cotd"):
        for c in range(chunks):
            cot_wait(diag, c)
    with scope("grad3"):
        gt[...] += dot_t(wb[diag], cb[diag])
        for h in range(heads):
            do_t = gt[h * HEAD : (h + 1) * HEAD].astype(BF16)
            dot_b[h] = do_t
            do_b[h] = do_t.T
            delta[h] = jnp.sum(do_t.astype(F32) * attn_t[h].astype(F32), axis=0, keepdims=True)

    def bwd_group(places, group):
        weights = [[] for _ in places]
        grads = [[] for _ in places]
        for h in range(heads):
            f = jnp.exp2(mg[group, h] - mrun[h]) * linv[h]
            for n, place in enumerate(places):
                p = pb[place, h].astype(F32) * f
                weights[n].append(p.astype(BF16))
                ds = (p * (dot(kv[place, 1], dot_b[h]) - delta[h])).astype(BF16)
                pb[place, h] = ds
                grads[n].append(ds)
        out = []
        for n in range(len(places)):
            dv = dot(jnp.concatenate(weights[n], axis=1), do_b[...].reshape(heads * rows, HEAD))
            dk = dot(jnp.concatenate(grads[n], axis=1), qs[...].reshape(heads * rows, HEAD))
            out.append((dk * scale, dv))
        return out

    def grad_relay(side):
        return send(
            gkv.at[7 + side], relay.at[side], rs.at[side], rr.at[side], peer(2 * side - 1), t
        )

    def grad_near(side, j):
        return send(
            gkv.at[3 + 2 * side + j],
            rx.at[side, j],
            gs.at[side, j],
            gr.at[side, j],
            peer(2 * side - 1),
            t,
        )

    def bwd_step(k, carry):
        j_up = jnp.where(k == 1, 1 - last, last)
        j_down = jnp.where(k == 1, first, 1 - first)
        places = [jnp.where(k == 0, 7, 3 + j_up), jnp.where(k == 0, 8, 5 + j_down)]
        with scope("bwd"):
            outs = bwd_group(places, jnp.where(k == 0, 2, 1))

        @pl.when(k < 2)
        def _():
            for place, (dk, dv) in zip(places, outs):
                gkv[place, 0] = dk.astype(BF16)
                gkv[place, 1] = dv.astype(BF16)

        @pl.when(k == 2)
        def _():
            for side, (place, (dk, dv)) in enumerate(zip(places, outs)):
                with scope("waitrelay"):
                    grad_relay(side).wait_recv()
                gkv[place, 0] = (dk + relay[side, 0].astype(F32)).astype(BF16)
                gkv[place, 1] = (dv + relay[side, 1].astype(F32)).astype(BF16)

        @pl.when(k == 0)
        def _():
            grad_relay(0).start()
            grad_relay(1).start()

        @pl.when(k > 0)
        def _():
            grad_near(0, j_up).start()
            grad_near(1, j_down).start()

        return carry

    lax.fori_loop(0, 3, bwd_step, 0)

    with scope("bwdown"):
        for n, (dk, dv) in enumerate(bwd_group([0, 1, 2], 0)):
            g3[n, 0] = dk
            g3[n, 1] = dv

    with scope("partner"):
        for c in range(chunks):
            pp[1, c] = part(partner, c).astype(BF16)
            to_partner(1, c).start()
        for c in range(chunks):
            po[c] = part(t, c)

    for side, e in enumerate((1, 3)):
        base = lax.div(x + e, GROUP)
        for j in range(2):
            with scope("gradnear"):
                grad_near(side, j).wait_recv()
            g3[base + j] = g3[base + j] + rx[side, j].astype(F32)

    def grad_far(k):
        return send(gkv.at[k + 1], rz.at[k], zs.at[k], zr.at[k], ctx_at(-4 * k - 4), t)

    for k in range(2):
        gkv[k + 1] = g3[k + 1].astype(BF16)
        grad_far(k).start()

    with scope("dq"):
        for n in range(SLOTS):
            ktb[:, n * rows : (n + 1) * rows] = kv[n, 0].T
        for h in range(heads):
            dq_t = dot(ktb[...], pb[:, h].reshape(SLOTS * rows, rows))
            gq[:, h * HEAD : (h + 1) * HEAD] = (dq_t * scale).T.astype(BF16)
    for c in range(chunks):
        with scope("rscross"):
            to_partner(1, c).wait_recv()
            to_cross(c).wait_recv()
        mixed[:, c * 256 : (c + 1) * 256] = (
            po[c] + pr[1, c].astype(F32) + xr[c].astype(F32)
        ).astype(BF16)
    for k in range(2):
        with scope("gradfar"):
            grad_far(k).wait_recv()
    total = g3[0] + rz[0].astype(F32) + rz[1].astype(F32)
    gk[...] = total[0].astype(BF16)
    gv[...] = total[1].astype(BF16)

    for place in range(1, SLOTS):
        near(0, place, 1).wait_send()
    for side in range(2):
        grad_relay(side).wait_send()
        for j in range(2):
            grad_near(side, j).wait_send()
    for k in range(2):
        grad_far(k).wait_send()
    for c in range(chunks):
        cot_send(c, cross, 0).wait_send()
        cot_send(c, partner, 1).wait_send()
        cot_pass(c).wait_send()
        to_partner(0, c).wait_send()
        to_partner(1, c).wait_send()
        to_cross(c).wait_send()


def leave(*refs):
    count = (len(refs) - 1) // 2
    sem = refs[-1]
    copies = [
        pltpu.make_async_copy(refs[n], refs[count + n], sem.at[n]) for n in range(count)
    ]
    for copy in copies:
        copy.start()
    for copy in copies:
        copy.wait()


def on_device(queries, keys, values, out_weight, cotangent, doc_ids):
    n_ctx = lax.axis_size("ctx")
    rows = queries.shape[0]
    heads = queries.shape[1] // HEAD
    chunks = cotangent.shape[1] // 256
    any_space = pl.BlockSpec(memory_space=pl.ANY)
    hbm = pl.BlockSpec(memory_space=pltpu.HBM)
    vmem = pl.BlockSpec(memory_space=pltpu.VMEM)
    dma = pltpu.SemaphoreType.DMA
    shapes = tuple(
        jax.ShapeDtypeStruct(like.shape, BF16) for like in (cotangent, queries, keys, values)
    )
    results = pl.pallas_call(
        functools.partial(kernel, n_ctx, heads, rows, chunks),
        out_shape=shapes,
        in_specs=[hbm] * 6,
        out_specs=(vmem,) * 4,
        scratch_shapes=[
            pltpu.SMEM(doc_ids.shape, jnp.int32),
            pltpu.VMEM((rows, heads * HEAD), BF16),
            pltpu.VMEM((heads, rows, HEAD), BF16),
            pltpu.VMEM((SLOTS, 2, rows, HEAD), BF16),
            pltpu.VMEM((4, heads * HEAD, chunks * 256), BF16),
            pltpu.VMEM((4, rows, chunks * 256), BF16),
            pltpu.VMEM((heads, HEAD, rows), BF16),
            pltpu.VMEM((4, heads, rows, rows), F32),
            pltpu.VMEM((SLOTS, heads, rows, rows), BF16),
            pltpu.VMEM((3, heads, 1, rows), F32),
            pltpu.VMEM((heads, 8, rows), F32),
            pltpu.VMEM((heads, 1, rows), F32),
            pltpu.VMEM((heads, 8, rows), F32),
            pltpu.VMEM((heads, 1, rows), F32),
            pltpu.VMEM((heads, HEAD, rows), F32),
            pltpu.VMEM((heads, HEAD, rows), BF16),
            pltpu.VMEM((rows, heads * HEAD), BF16),
            pltpu.VMEM((heads * HEAD, rows), F32),
            pltpu.VMEM((heads, HEAD, rows), BF16),
            pltpu.VMEM((heads, rows, HEAD), BF16),
            pltpu.VMEM((heads, 1, rows), F32),
            pltpu.VMEM((HEAD, SLOTS * rows), BF16),
            pltpu.VMEM((SLOTS, 2, rows, HEAD), BF16),
            pltpu.VMEM((3, 2, rows, HEAD), F32),
            pltpu.VMEM((2, 2, rows, HEAD), BF16),
            pltpu.VMEM((2, 2, 2, rows, HEAD), BF16),
            pltpu.VMEM((2, 2, rows, HEAD), BF16),
            pltpu.VMEM((2, chunks, rows, 256), BF16),
            pltpu.VMEM((2, chunks, rows, 256), BF16),
            pltpu.VMEM((chunks, rows, 256), BF16),
            pltpu.VMEM((chunks, rows, 256), BF16),
            pltpu.VMEM((chunks, rows, 256), F32),
            dma,
            dma,
            dma((2,)),
            dma((4,)),
            dma,
            dma((SLOTS,)),
            dma((SLOTS,)),
            dma((3, chunks)),
            dma((4, chunks)),
            dma((2,)),
            dma((2,)),
            dma((2, 2)),
            dma((2, 2)),
            dma((2,)),
            dma((2,)),
            dma((2, chunks)),
            dma((2, chunks)),
            dma((chunks,)),
            dma((chunks,)),
        ],
        compiler_params=pltpu.CompilerParams(
            collective_id=0, has_side_effects=True, vmem_limit_bytes=50 * 1024 * 1024
        ),
    )(
        *[
            pltpu.with_memory_space_constraint(a, pltpu.HBM)
            for a in (doc_ids, queries, keys, values, out_weight, cotangent)
        ]
    )
    return pl.pallas_call(
        leave,
        out_shape=shapes,
        in_specs=[any_space] * 4,
        out_specs=(any_space,) * 4,
        scratch_shapes=[dma((4,))],
        compiler_params=pltpu.CompilerParams(vmem_limit_bytes=1024 * 1024),
    )(*results)


def solution(mesh):
    return jax.shard_map(
        on_device,
        mesh=mesh,
        in_specs=(
            P("ctx", "tp"),
            P("ctx", "tp"),
            P("ctx", "tp"),
            P("tp", None),
            P("ctx", "tp"),
            P(),
        ),
        out_specs=(P("ctx", "tp"), P("ctx", "tp"), P("ctx", "tp"), P("ctx", "tp")),
        check_vma=False,
    )
```

time: 76.5 us -> 55 us (0.72)
  the two profiles are of different devices: /device:TPU:4 before, /device:TPU:1 now
where the time goes in v2:
time: 55 us; the launch traced here: 54.9 us
  Pallas kernels  54.1 us (98%)
  between operations  0.8 us (1%)
    pallas_call x1, Pallas kernels, on_device(): pl.pallas_call(functools.partial(kernel, n_ctx, heads, rows, chunks), out...  53.1 us

profile of v2, /device:TPU:1, one launch (start us, length us, event | category | flops | bytes accessed | tf_op | source)
XLA Modules:
  0.0 54.9 jit_solution(15846777484070264189)
XLA Ops:
  0.6 53.1 %shard_map.93 = (bf16[256,1280]{1,0:T(8,128)(2,1)S(1)}, bf16[256,640]{1,0:T(8,128)(2,1)S(1)}, bf16[256,128]{1,0:T(8,128)(2,1)S(1)}, bf16[256,128]{1,0:T(8,128)(2,1)S(1)}) custom-call(s32[128]{0:T(128)} %doc_in.1, bf16[256,640]{1,0:T(8,128)(2,1)} %q_in.1, bf16[256,128]{1,0:T(8,128)(2,1)} %k_in.1, bf16[256,128]{1,0:T(8,128)(2,1)} %v_in.1, ...), custom_call_target="tpu_custom_call" | custom-call | tf_op jit(solution)/shard_map/pallas_call | solution.py:539
  53.7 1.0 %shard_map.94 = (bf16[256,1280]{1,0:T(8,128)(2,1)}, bf16[256,640]{1,0:T(8,128)(2,1)}, bf16[256,128]{1,0:T(8,128)(2,1)}, bf16[256,128]{1,0:T(8,128)(2,1)}) custom-call(bf16[256,1280]{1,0:T(8,128)(2,1)S(1)} %get-tuple-element.8.refs_0_, bf16[256,640]{1,0:T(8,128)(2,1)S(1)} %get-tuple-element.9.refs_1_, bf16[256,128]{1,0:T(8,128)(2,1)S(1)} %get-tuple-element.10.refs_2_, ...), custom_call_target="tpu_custom_call" | custom-call | tf_op jit(solution)/shard_map/pallas_call | solution.py:606

commit v3 on v2

--- a/solution.py
+++ b/solution.py
@@ -42,10 +42,15 @@
     v_in,
     w_in,
     c_in,
+    mixed_out,
+    gq_out,
+    gk_out,
+    gv_out,
     mixed,
     gq,
     gk,
     gv,
+    out_sem,
     doc,
     qb,
     qs,
@@ -87,11 +92,9 @@
     kr,
     cs,
     cr,
-    rs,
     rr,
     gs,
     gr,
-    zs,
     zr,
     ps,
     prs,
@@ -116,6 +119,14 @@
     def peer(e):
         return g0 + lax.rem(x + e + GROUP, GROUP)
 
+    barrier = pltpu.get_barrier_semaphore()
+    for by in (4, -4, 8, -8):
+        pl.semaphore_signal(barrier, inc=1, device_id=(ctx_at(by), t), device_id_type=MESH)
+    for e in (1, 3):
+        pl.semaphore_signal(barrier, inc=1, device_id=(peer(e), t), device_id_type=MESH)
+    for other in (partner, cross):
+        pl.semaphore_signal(barrier, inc=1, device_id=(i, other), device_id_type=MESH)
+
     own_k = pltpu.make_async_copy(k_in, kv.at[0, 0], o_sem.at[0])
     own_v = pltpu.make_async_copy(v_in, kv.at[0, 1], o_sem.at[1])
     own_k.start()
@@ -136,13 +147,6 @@
     for s in (t, partner, diag, cross):
         w_copy(s).start()
 
-    barrier = pltpu.get_barrier_semaphore()
-    for by in (4, -4, 8, -8):
-        pl.semaphore_signal(barrier, inc=1, device_id=(ctx_at(by), t), device_id_type=MESH)
-    for e in (1, 3):
-        pl.semaphore_signal(barrier, inc=1, device_id=(peer(e), t), device_id_type=MESH)
-    for other in (partner, cross):
-        pl.semaphore_signal(barrier, inc=1, device_id=(i, other), device_id_type=MESH)
     with scope("barrier"):
         pl.semaphore_wait(barrier, 8)
 
@@ -156,41 +160,43 @@
             device_id_type=MESH,
         )
 
-    def far(place):
-        return send(kv.at[0], kv.at[place], ks.at[place], kr.at[place], ctx_at(4 * place), t)
-
-    def near(src, place, e):
-        return send(kv.at[src], kv.at[place], ks.at[place], kr.at[place], peer(e), t)
-
-    def arrived(place):
-        near(0, place, 1).wait_recv()
+    def kv_send(src, place, b, ctx):
+        return send(kv.at[src, b], kv.at[place, b], ks, kr.at[place, b], ctx, t)
+
+    def far(place, b):
+        return kv_send(0, place, b, ctx_at(4 * place))
+
+    def near(src, place, e, b):
+        return kv_send(src, place, b, peer(e))
+
+    def arrived(place, b):
+        near(0, place, 1, b).wait_recv()
 
     def cot_send(c, to, k):
         cols = pl.ds(c * 256, 256)
-        return send(c_in.at[:, cols], cb.at[t, :, cols], cs.at[k, c], cr.at[t, c], i, to)
+        return send(c_in.at[:, cols], cb.at[t, :, cols], cs, cr.at[k], i, to)
 
     def cot_pass(c):
         cols = pl.ds(c * 256, 256)
         block = cb.at[cross, :, cols]
-        return send(block, block, cs.at[2, c], cr.at[cross, c], i, partner)
-
-    def cot_wait(s, c):
-        cols = pl.ds(c * 256, 256)
-        block = cb.at[s, :, cols]
-        send(block, block, cs.at[0, c], cr.at[s, c], i, partner).wait_recv()
-
-    own_k.wait()
-    own_v.wait()
-    far(1).start()
-    far(2).start()
-    for e in (1, 3):
-
-        @pl.when(x + e < GROUP)
-        def _():
-            near(0, 2 + e, e).start()
+        return send(block, block, cs, cr.at[6 if c < 3 else 7], i, partner)
+
+    def cot_wait(s, lo, hi, k):
+        block = cb.at[s, :, pl.ds(lo * 256, (hi - lo) * 256)]
+        send(block, block, cs, cr.at[k], i, partner).wait_recv()
+
+    for b, own in enumerate((own_k, own_v)):
+        own.wait()
+        far(1, b).start()
+        far(2, b).start()
+        for e in (1, 3):
+
+            @pl.when(x + e < GROUP)
+            def _():
+                near(0, 2 + e, e, b).start()
 
     for c in range(chunks):
-        cot_send(c, partner, 1).start()
+        cot_send(c, partner, 5).start()
 
     q_copy.wait()
     doc_copy.wait()
@@ -268,48 +274,65 @@
     with scope("slot0"):
         scores(0, 0, None)
     for c in range(chunks):
-        cot_send(c, cross, 0).start()
+        cot_send(c, cross, c).start()
     with scope("grad0"):
         w_copy(t).wait()
         own_c.wait()
         gt[...] = dot_t(wb[t], cb[t])
-    with scope("wait4"):
-        far(1).wait_recv()
-    for e in (1, 3):
-
-        @pl.when(x + e < GROUP)
+    for b in range(2):
+        with scope("wait8"):
+            arrived(2, b)
+
+        @pl.when(x >= 2)
         def _():
-            near(1, 3 + e, e).start()
-
-        @pl.when(x + e >= GROUP)
+            near(2, 6, 3, b).start()
+
+        if b == 0:
+            with scope("grad1"):
+                w_copy(partner).wait()
+                cot_wait(partner, 0, chunks, 5)
+                gt[...] += dot_t(wb[partner], cb[partner])
+
+    with scope("score8"):
+        scores(2, 2, 8)
+    for b in range(2):
+        with scope("wait4"):
+            arrived(1, b)
+
+        for e in (1, 3):
+
+            @pl.when(x + e < GROUP)
+            def _():
+                near(1, 3 + e, e, b).start()
+
+            @pl.when(x + e >= GROUP)
+            def _():
+                near(1, 2 + e, e, b).start()
+
+    for b in range(2):
+
+        @pl.when(x == 1)
         def _():
-            near(1, 2 + e, e).start()
-
-    with scope("wait8"):
-        far(2).wait_recv()
-    for e in (1, 3):
-
-        @pl.when(x + e >= GROUP)
+            near(2, 6, 3, b).start()
+
+        @pl.when(x == GROUP - 1)
         def _():
-            near(2, 3 + e, e).start()
-
+            near(2, 4, 1, b).start()
+
+    with scope("score4"):
+        scores(1, 1, 4)
+
+    up, down = 3 + last, 6 - first
+    for b in range(2):
+        with scope("waitup"):
+            arrived(up, b)
+        near(up, 7, 1, b).start()
     with scope("groupA"):
-        scores(1, 1, 4)
-        scores(2, 2, 8)
         weigh(0, [(0, None), (1, 4), (2, 8)])
-
-    up, down = 3 + last, 6 - first
-    with scope("waitup"):
-        arrived(up)
-    near(up, 7, 1).start()
-    with scope("waitdown"):
-        arrived(down)
-    near(down, 8, -1).start()
-    with scope("grad1"):
-        w_copy(partner).wait()
-        for c in range(chunks):
-            cot_wait(partner, c)
-        gt[...] += dot_t(wb[partner], cb[partner])
+    for b in range(2):
+        with scope("waitdown"):
+            arrived(down, b)
+        near(down, 8, -1, b).start()
     rest_up, rest_down = 4 - last, 5 + first
     group_b = [
         (up, 1 + 4 * last),
@@ -320,17 +343,33 @@
     for k, (place, d) in enumerate(group_b):
         if k >= 2:
             with scope("waitb"):
-                arrived(place)
+                arrived(place, 0)
         with scope("scoreb"):
             scores(k, place, d)
     with scope("groupB"):
+        arrived(rest_up, 1)
+        arrived(rest_down, 1)
         weigh(1, group_b)
+    for c in range(3):
+        with scope("cotx"):
+            cot_wait(cross, c, c + 1, c)
+        cot_pass(c).start()
+
+    def grad_piece(s, lo, hi):
+        cols = slice(lo * 256, hi * 256)
+        gt[...] += dot_t(wb[s, :, cols], cb[s, :, cols])
+
+    with scope("grad2"):
+        w_copy(cross).wait()
+        grad_piece(cross, 0, 3)
     group_c = [(7, 2), (8, 6)]
     for k, (place, d) in enumerate(group_c):
         with scope("waitc"):
-            arrived(place)
+            arrived(place, 0)
         scores(k, place, d)
     with scope("groupC"):
+        arrived(7, 1)
+        arrived(8, 1)
         weigh(2, group_c)
 
         for h in range(heads):
@@ -344,37 +383,46 @@
         return dot(attn[...], wb[s, :, c * 256 : (c + 1) * 256])
 
     def to_partner(k, c):
-        return send(pp.at[k, c], pr.at[k, c], ps.at[k, c], prs.at[k, c], i, partner)
+        return send(pp.at[k, c], pr.at[k, c], ps, prs.at[chunks if k else c], i, partner)
 
     def to_cross(c):
-        return send(xc.at[c], xr.at[c], xs.at[c], xrs.at[c], i, cross)
+        return send(xc.at[c], xr.at[c], xs, xrs, i, cross)
 
     with scope("diag"):
         w_copy(diag).wait()
         for c in range(chunks):
             pp[0, c] = part(diag, c).astype(BF16)
+        for c in range(2):
             to_partner(0, c).start()
+    for c in range(3, chunks):
+        with scope("cotx"):
+            cot_wait(cross, c, c + 1, c)
+        cot_pass(c).start()
+    for c in range(2, chunks):
+        to_partner(0, c).start()
+
+    def rs_step(lo, hi):
+        with scope("rs1"):
+            for c in range(lo, hi):
+                to_partner(0, c).wait_recv()
+                xc[c] = (po[c] + pr[0, c].astype(F32)).astype(BF16)
+                to_cross(c).start()
+
+    with scope("grad2"):
+        grad_piece(cross, 3, chunks)
+    with scope("cotd"):
+        cot_wait(diag, 0, 3, 6)
+    with scope("grad3"):
+        grad_piece(diag, 0, 3)
     with scope("cross"):
-        w_copy(cross).wait()
         for c in range(chunks):
             po[c] = part(cross, c)
-    with scope("rs1"):
-        for c in range(chunks):
-            to_partner(0, c).wait_recv()
-            xc[c] = (po[c] + pr[0, c].astype(F32)).astype(BF16)
-            to_cross(c).start()
-
-    with scope("cotx"):
-        for c in range(chunks):
-            cot_wait(cross, c)
-            cot_pass(c).start()
-    with scope("grad2"):
-        gt[...] += dot_t(wb[cross], cb[cross])
+    rs_step(0, 2)
     with scope("cotd"):
-        for c in range(chunks):
-            cot_wait(diag, c)
+        cot_wait(diag, 3, chunks, 7)
     with scope("grad3"):
-        gt[...] += dot_t(wb[diag], cb[diag])
+        grad_piece(diag, 3, chunks)
+    with scope("heads"):
         for h in range(heads):
             do_t = gt[h * HEAD : (h + 1) * HEAD].astype(BF16)
             dot_b[h] = do_t
@@ -392,24 +440,32 @@
                 ds = (p * (dot(kv[place, 1], dot_b[h]) - delta[h])).astype(BF16)
                 pb[place, h] = ds
                 grads[n].append(ds)
-        out = []
-        for n in range(len(places)):
-            dv = dot(jnp.concatenate(weights[n], axis=1), do_b[...].reshape(heads * rows, HEAD))
-            dk = dot(jnp.concatenate(grads[n], axis=1), qs[...].reshape(heads * rows, HEAD))
-            out.append((dk * scale, dv))
-        return out
-
-    def grad_relay(side):
+        def values_part(n):
+            w = jnp.concatenate(weights[n], axis=1)
+            return dot(w, do_b[...].reshape(heads * rows, HEAD))
+
+        def keys_part(n):
+            ds = jnp.concatenate(grads[n], axis=1)
+            return dot(ds, qs[...].reshape(heads * rows, HEAD)) * scale
+
+        return keys_part, values_part
+
+    def grad_relay(side, b):
         return send(
-            gkv.at[7 + side], relay.at[side], rs.at[side], rr.at[side], peer(2 * side - 1), t
+            gkv.at[7 + side, b],
+            relay.at[side, b],
+            gs,
+            rr.at[side, b],
+            peer(2 * side - 1),
+            t,
         )
 
-    def grad_near(side, j):
+    def grad_near(side, j, b):
         return send(
-            gkv.at[3 + 2 * side + j],
-            rx.at[side, j],
-            gs.at[side, j],
-            gr.at[side, j],
+            gkv.at[3 + 2 * side + j, b],
+            rx.at[side, j, b],
+            gs,
+            gr.at[side, j, b],
             peer(2 * side - 1),
             t,
         )
@@ -419,61 +475,84 @@
         j_down = jnp.where(k == 1, first, 1 - first)
         places = [jnp.where(k == 0, 7, 3 + j_up), jnp.where(k == 0, 8, 5 + j_down)]
         with scope("bwd"):
-            outs = bwd_group(places, jnp.where(k == 0, 2, 1))
-
-        @pl.when(k < 2)
-        def _():
-            for place, (dk, dv) in zip(places, outs):
-                gkv[place, 0] = dk.astype(BF16)
-                gkv[place, 1] = dv.astype(BF16)
-
-        @pl.when(k == 2)
-        def _():
-            for side, (place, (dk, dv)) in enumerate(zip(places, outs)):
-                with scope("waitrelay"):
-                    grad_relay(side).wait_recv()
-                gkv[place, 0] = (dk + relay[side, 0].astype(F32)).astype(BF16)
-                gkv[place, 1] = (dv + relay[side, 1].astype(F32)).astype(BF16)
-
-        @pl.when(k == 0)
-        def _():
-            grad_relay(0).start()
-            grad_relay(1).start()
-
-        @pl.when(k > 0)
-        def _():
-            grad_near(0, j_up).start()
-            grad_near(1, j_down).start()
+            parts = bwd_group(places, jnp.where(k == 0, 2, 1))
+        for b in (1, 0):
+            with scope("bwdpart"):
+                done = [parts[b](n) for n in range(2)]
+
+            @pl.when(k < 2)
+            def _():
+                for side, place in enumerate(places):
+                    gkv[place, b] = done[side].astype(BF16)
+
+            @pl.when(k == 2)
+            def _():
+                for side, place in enumerate(places):
+                    with scope("waitrelay"):
+                        grad_relay(side, b).wait_recv()
+                    gkv[place, b] = (done[side] + relay[side, b].astype(F32)).astype(BF16)
+
+            @pl.when(k == 0)
+            def _():
+                grad_relay(0, b).start()
+                grad_relay(1, b).start()
+                if b == 1:
+                    rs_step(2, chunks)
+
+            @pl.when(k > 0)
+            def _():
+                grad_near(0, j_up, b).start()
+                grad_near(1, j_down, b).start()
 
         return carry
 
     lax.fori_loop(0, 3, bwd_step, 0)
 
     with scope("bwdown"):
-        for n, (dk, dv) in enumerate(bwd_group([0, 1, 2], 0)):
-            g3[n, 0] = dk
-            g3[n, 1] = dv
+        parts = bwd_group([0, 1, 2], 0)
+        for n in range(3):
+            for b in range(2):
+                g3[n, b] = parts[b](n)
 
     with scope("partner"):
         for c in range(chunks):
             pp[1, c] = part(partner, c).astype(BF16)
+        for c in range(chunks):
             to_partner(1, c).start()
+
+    def grad_far(k, b):
+        return send(
+            gkv.at[k + 1, b], rz.at[k, b], gs, zr.at[k, b], ctx_at(-4 * k - 4), t
+        )
+
+    def near_sum(k, b):
+        total = g3[k, b]
+        for side, e in enumerate((1, 3)):
+            j = k - lax.div(x + e, GROUP)
+            block = rx[side, jnp.clip(j, 0, 1), b].astype(F32)
+            total = total + jnp.where((j >= 0) & (j <= 1), block, 0.0)
+        return total
+
+    for b in (1, 0):
+        with scope("gradnear"):
+            for side in range(2):
+                for j in range(2):
+                    grad_near(side, j, b).wait_recv()
+        with scope("nearsum"):
+            for k in range(2):
+                gkv[k + 1, b] = near_sum(k + 1, b).astype(BF16)
+                grad_far(k, b).start()
+
+    with scope("ownpart"):
         for c in range(chunks):
             po[c] = part(t, c)
-
-    for side, e in enumerate((1, 3)):
-        base = lax.div(x + e, GROUP)
-        for j in range(2):
-            with scope("gradnear"):
-                grad_near(side, j).wait_recv()
-            g3[base + j] = g3[base + j] + rx[side, j].astype(F32)
-
-    def grad_far(k):
-        return send(gkv.at[k + 1], rz.at[k], zs.at[k], zr.at[k], ctx_at(-4 * k - 4), t)
-
-    for k in range(2):
-        gkv[k + 1] = g3[k + 1].astype(BF16)
-        grad_far(k).start()
+    for b in range(2):
+        g3[0, b] = near_sum(0, b)
+
+    def put(n):
+        src = (mixed, gq, gv, gk)[n]
+        dst = (mixed_out, gq_out, gv_out, gk_out)[n]
+        return pltpu.make_async_copy(src, dst, out_sem.at[n])
 
     with scope("dq"):
         for n in range(SLOTS):
@@ -481,35 +560,34 @@
         for h in range(heads):
             dq_t = dot(ktb[...], pb[:, h].reshape(SLOTS * rows, rows))
             gq[:, h * HEAD : (h + 1) * HEAD] = (dq_t * scale).T.astype(BF16)
+    put(1).start()
+    with scope("rscross"):
+        send(pp.at[1], pr.at[1], ps, prs.at[chunks], i, partner).wait_recv()
+        send(xc, xr, xs, xrs, i, cross).wait_recv()
     for c in range(chunks):
-        with scope("rscross"):
-            to_partner(1, c).wait_recv()
-            to_cross(c).wait_recv()
         mixed[:, c * 256 : (c + 1) * 256] = (
             po[c] + pr[1, c].astype(F32) + xr[c].astype(F32)
         ).astype(BF16)
-    for k in range(2):
-        with scope("gradfar"):
-            grad_far(k).wait_recv()
-    total = g3[0] + rz[0].astype(F32) + rz[1].astype(F32)
-    gk[...] = total[0].astype(BF16)
-    gv[...] = total[1].astype(BF16)
-
-    for place in range(1, SLOTS):
-        near(0, place, 1).wait_send()
-    for side in range(2):
-        grad_relay(side).wait_send()
-        for j in range(2):
-            grad_near(side, j).wait_send()
-    for k in range(2):
-        grad_far(k).wait_send()
-    for c in range(chunks):
-        cot_send(c, cross, 0).wait_send()
-        cot_send(c, partner, 1).wait_send()
-        cot_pass(c).wait_send()
-        to_partner(0, c).wait_send()
-        to_partner(1, c).wait_send()
-        to_cross(c).wait_send()
+    put(0).start()
+    with scope("sent"):
+        block = kv.at[pl.ds(1, SLOTS - 1)]
+        send(block, block, ks, kr.at[0, 0], i, partner).wait_send()
+        block = cb.at[pl.ds(0, 3)]
+        send(block, block, cs, cr.at[0], i, partner).wait_send()
+        send(pp, pr, ps, prs.at[0], i, partner).wait_send()
+        send(xc, xr, xs, xrs, i, cross).wait_send()
+    for b, result in ((1, gv), (0, gk)):
+        for k in range(2):
+            with scope("gradfar"):
+                grad_far(k, b).wait_recv()
+        result[...] = (g3[0, b] + rz[0, b].astype(F32) + rz[1, b].astype(F32)).astype(BF16)
+        put(3 - b).start()
+
+    with scope("put"):
+        for n in range(4):
+            put(n).wait()
+        block = gkv.at[pl.ds(1, SLOTS - 1)]
+        send(block, block, gs, zr.at[0, 0], i, partner).wait_send()
 
 
 def leave(*refs):
@@ -531,7 +609,6 @@
     chunks = cotangent.shape[1] // 256
     any_space = pl.BlockSpec(memory_space=pl.ANY)
     hbm = pl.BlockSpec(memory_space=pltpu.HBM)
-    vmem = pl.BlockSpec(memory_space=pltpu.VMEM)
     dma = pltpu.SemaphoreType.DMA
     shapes = tuple(
         jax.ShapeDtypeStruct(like.shape, BF16) for like in (cotangent, queries, keys, values)
@@ -540,8 +617,10 @@
         functools.partial(kernel, n_ctx, heads, rows, chunks),
         out_shape=shapes,
         in_specs=[hbm] * 6,
-        out_specs=(vmem,) * 4,
+        out_specs=(any_space,) * 4,
         scratch_shapes=[
+            *[pltpu.VMEM(shape.shape, BF16) for shape in shapes],
+            dma((4,)),
             pltpu.SMEM(doc_ids.shape, jnp.int32),
             pltpu.VMEM((rows, heads * HEAD), BF16),
             pltpu.VMEM((heads, rows, HEAD), BF16),
@@ -579,20 +658,18 @@
             dma((2,)),
             dma((4,)),
             dma,
-            dma((SLOTS,)),
-            dma((SLOTS,)),
-            dma((3, chunks)),
-            dma((4, chunks)),
-            dma((2,)),
-            dma((2,)),
+            dma,
+            dma((SLOTS, 2)),
+            dma,
+            dma((8,)),
             dma((2, 2)),
+            dma,
+            dma((2, 2, 2)),
             dma((2, 2)),
-            dma((2,)),
-            dma((2,)),
-            dma((2, chunks)),
-            dma((2, chunks)),
-            dma((chunks,)),
-            dma((chunks,)),
+            dma,
+            dma((chunks + 1,)),
+            dma,
+            dma,
         ],
         compiler_params=pltpu.CompilerParams(
             collective_id=0, has_side_effects=True, vmem_limit_bytes=50 * 1024 * 1024

time: 55 us -> 54 us (0.982)
  Pallas kernels: 54.1 us -> 53.1 us
    pallas_call x1, Pallas kernels: 53.1 us -> 52.1 us  [on_device(): pl.pallas_call(functools.partial(kernel, n_ctx, heads, rows, chunks), out...]
where the time goes in v3:
time: 54 us; the launch traced here: 53.9 us
  Pallas kernels  53.1 us (98%)
  between operations  0.8 us (1%)
    pallas_call x1, Pallas kernels, on_device(): pl.pallas_call(functools.partial(kernel, n_ctx, heads, rows, chunks), out...  52.1 us

profile of v3, /device:TPU:1, one launch (start us, length us, event | category | flops | bytes accessed | tf_op | source)
XLA Modules:
  0.0 53.9 jit_solution(4877544256161781432)
XLA Ops:
  0.6 52.1 %shard_map.93 = (bf16[256,1280]{1,0:T(8,128)(2,1)S(1)}, bf16[256,640]{1,0:T(8,128)(2,1)S(1)}, bf16[256,128]{1,0:T(8,128)(2,1)S(1)}, bf16[256,128]{1,0:T(8,128)(2,1)S(1)}) custom-call(s32[128]{0:T(128)} %doc_in.1, bf16[256,640]{1,0:T(8,128)(2,1)} %q_in.1, bf16[256,128]{1,0:T(8,128)(2,1)} %k_in.1, bf16[256,128]{1,0:T(8,128)(2,1)} %v_in.1, ...), custom_call_target="tpu_custom_call" | custom-call | tf_op jit(solution)/shard_map/pallas_call | solution.py:616
  52.7 1.0 %shard_map.94 = (bf16[256,1280]{1,0:T(8,128)(2,1)}, bf16[256,640]{1,0:T(8,128)(2,1)}, bf16[256,128]{1,0:T(8,128)(2,1)}, bf16[256,128]{1,0:T(8,128)(2,1)}) custom-call(bf16[256,1280]{1,0:T(8,128)(2,1)S(1)} %get-tuple-element.8.refs_0_, bf16[256,640]{1,0:T(8,128)(2,1)S(1)} %get-tuple-element.9.refs_1_, bf16[256,128]{1,0:T(8,128)(2,1)S(1)} %get-tuple-element.10.refs_2_, ...), custom_call_target="tpu_custom_call" | custom-call | tf_op jit(solution)/shard_map/pallas_call | solution.py:683

commit v4 on v3

--- a/solution.py
+++ b/solution.py
@@ -89,6 +89,7 @@
     w_sem,
     c_sem,
     ks,
+    kp,
     kr,
     cs,
     cr,
@@ -122,7 +123,7 @@
     barrier = pltpu.get_barrier_semaphore()
     for by in (4, -4, 8, -8):
         pl.semaphore_signal(barrier, inc=1, device_id=(ctx_at(by), t), device_id_type=MESH)
-    for e in (1, 3):
+    for e in (1, 2, 3):
         pl.semaphore_signal(barrier, inc=1, device_id=(peer(e), t), device_id_type=MESH)
     for other in (partner, cross):
         pl.semaphore_signal(barrier, inc=1, device_id=(i, other), device_id_type=MESH)
@@ -148,7 +149,7 @@
         w_copy(s).start()
 
     with scope("barrier"):
-        pl.semaphore_wait(barrier, 8)
+        pl.semaphore_wait(barrier, 9)
 
     def send(src, dst, s_sem, r_sem, ctx, tp):
         return pltpu.make_async_remote_copy(
@@ -168,6 +169,12 @@
 
     def near(src, place, e, b):
         return kv_send(src, place, b, peer(e))
+
+    def pass_on(src, place, e, b):
+        block = kv.at[place, b]
+        return send(kv.at[src, b], block, kp.at[place - 7, b], kr.at[place, b], peer(e), t)
+
+    middle = (x >= 1) & (x <= 2)
 
     def arrived(place, b):
         near(0, place, 1, b).wait_recv()
@@ -293,6 +300,13 @@
                 cot_wait(partner, 0, chunks, 5)
                 gt[...] += dot_t(wb[partner], cb[partner])
 
+    for b in range(2):
+
+        @pl.when(middle)
+        def _():
+            arrived(3, b)
+            pass_on(3, 7, 1, b).start()
+
     with scope("score8"):
         scores(2, 2, 8)
     for b in range(2):
@@ -309,6 +323,8 @@
             def _():
                 near(1, 2 + e, e, b).start()
 
+        near(1, 8 - lax.div(x, 2), 2, b).start()
+
     for b in range(2):
 
         @pl.when(x == 1)
@@ -324,15 +340,21 @@
 
     up, down = 3 + last, 6 - first
     for b in range(2):
-        with scope("waitup"):
-            arrived(up, b)
-        near(up, 7, 1, b).start()
+
+        @pl.when(middle)
+        def _():
+            arrived(6, b)
+            pass_on(6, 8, -1, b).start()
+
     with scope("groupA"):
         weigh(0, [(0, None), (1, 4), (2, 8)])
     for b in range(2):
-        with scope("waitdown"):
+
+        @pl.when(jnp.logical_not(middle))
+        def _():
+            arrived(up, b)
             arrived(down, b)
-        near(down, 8, -1, b).start()
+
     rest_up, rest_down = 4 - last, 5 + first
     group_b = [
         (up, 1 + 4 * last),
@@ -570,8 +592,15 @@
         ).astype(BF16)
     put(0).start()
     with scope("sent"):
-        block = kv.at[pl.ds(1, SLOTS - 1)]
+        block = kv.at[pl.ds(1, SLOTS - 2)]
         send(block, block, ks, kr.at[0, 0], i, partner).wait_send()
+
+        @pl.when(middle)
+        def _():
+            for b in range(2):
+                pass_on(3, 7, 1, b).wait_send()
+                pass_on(6, 8, -1, b).wait_send()
+
         block = cb.at[pl.ds(0, 3)]
         send(block, block, cs, cr.at[0], i, partner).wait_send()
         send(pp, pr, ps, prs.at[0], i, partner).wait_send()
@@ -659,6 +688,7 @@
             dma((4,)),
             dma,
             dma,
+            dma((2, 2)),
             dma((SLOTS, 2)),
             dma,
             dma((8,)),

time: 54 us -> 55.3 us (1.024)
  Pallas kernels: 53.1 us -> 54.4 us
    pallas_call x1, Pallas kernels: 52.1 us -> 53.4 us  [on_device(): pl.pallas_call(functools.partial(kernel, n_ctx, heads, rows, chunks), out...]
where the time goes in v4:
time: 55.3 us; the launch traced here: 55.2 us
  Pallas kernels  54.4 us (98%)
  between operations  0.8 us (1%)
    pallas_call x1, Pallas kernels, on_device(): pl.pallas_call(functools.partial(kernel, n_ctx, heads, rows, chunks), out...  53.4 us

profile of v4, /device:TPU:1, one launch (start us, length us, event | category | flops | bytes accessed | tf_op | source)
XLA Modules:
  0.0 55.2 jit_solution(9021809093547193161)
XLA Ops:
  0.6 53.4 %shard_map.93 = (bf16[256,1280]{1,0:T(8,128)(2,1)S(1)}, bf16[256,640]{1,0:T(8,128)(2,1)S(1)}, bf16[256,128]{1,0:T(8,128)(2,1)S(1)}, bf16[256,128]{1,0:T(8,128)(2,1)S(1)}) custom-call(s32[128]{0:T(128)} %doc_in.1, bf16[256,640]{1,0:T(8,128)(2,1)} %q_in.1, bf16[256,128]{1,0:T(8,128)(2,1)} %k_in.1, bf16[256,128]{1,0:T(8,128)(2,1)} %v_in.1, ...), custom_call_target="tpu_custom_call" | custom-call | tf_op jit(solution)/shard_map/pallas_call | solution.py:645
  54.1 1.0 %shard_map.94 = (bf16[256,1280]{1,0:T(8,128)(2,1)}, bf16[256,640]{1,0:T(8,128)(2,1)}, bf16[256,128]{1,0:T(8,128)(2,1)}, bf16[256,128]{1,0:T(8,128)(2,1)}) custom-call(bf16[256,1280]{1,0:T(8,128)(2,1)S(1)} %get-tuple-element.8.refs_0_, bf16[256,640]{1,0:T(8,128)(2,1)S(1)} %get-tuple-element.9.refs_1_, bf16[256,128]{1,0:T(8,128)(2,1)S(1)} %get-tuple-element.10.refs_2_, ...), custom_call_target="tpu_custom_call" | custom-call | tf_op jit(solution)/shard_map/pallas_call | solution.py:713

commit v5 on v3

--- a/solution.py
+++ b/solution.py
@@ -363,15 +363,14 @@
         w_copy(cross).wait()
         grad_piece(cross, 0, 3)
     group_c = [(7, 2), (8, 6)]
-    for k, (place, d) in enumerate(group_c):
+    for n, (place, d) in enumerate(group_c):
         with scope("waitc"):
             arrived(place, 0)
-        scores(k, place, d)
-    with scope("groupC"):
-        arrived(7, 1)
-        arrived(8, 1)
-        weigh(2, group_c)
-
+        scores(0, place, d)
+        arrived(place, 1)
+        with scope("groupC"):
+            weigh(2 + n, [(place, d)])
+    with scope("attn"):
         for h in range(heads):
             inv = 1.0 / jnp.sum(l8[h], axis=0, keepdims=True)
             linv[h] = inv
@@ -429,12 +428,12 @@
             do_b[h] = do_t.T
             delta[h] = jnp.sum(do_t.astype(F32) * attn_t[h].astype(F32), axis=0, keepdims=True)
 
-    def bwd_group(places, group):
+    def bwd_group(places, groups):
         weights = [[] for _ in places]
         grads = [[] for _ in places]
         for h in range(heads):
-            f = jnp.exp2(mg[group, h] - mrun[h]) * linv[h]
             for n, place in enumerate(places):
+                f = jnp.exp2(mg[groups[n], h] - mrun[h]) * linv[h]
                 p = pb[place, h].astype(F32) * f
                 weights[n].append(p.astype(BF16))
                 ds = (p * (dot(kv[place, 1], dot_b[h]) - delta[h])).astype(BF16)
@@ -475,7 +474,7 @@
         j_down = jnp.where(k == 1, first, 1 - first)
         places = [jnp.where(k == 0, 7, 3 + j_up), jnp.where(k == 0, 8, 5 + j_down)]
         with scope("bwd"):
-            parts = bwd_group(places, jnp.where(k == 0, 2, 1))
+            parts = bwd_group(places, [jnp.where(k == 0, 2 + n, 1) for n in range(2)])
         for b in (1, 0):
             with scope("bwdpart"):
                 done = [parts[b](n) for n in range(2)]
@@ -509,7 +508,7 @@
     lax.fori_loop(0, 3, bwd_step, 0)
 
     with scope("bwdown"):
-        parts = bwd_group([0, 1, 2], 0)
+        parts = bwd_group([0, 1, 2], [0] * 3)
         for n in range(3):
             for b in range(2):
                 g3[n, b] = parts[b](n)
@@ -630,7 +629,7 @@
             pltpu.VMEM((heads, HEAD, rows), BF16),
             pltpu.VMEM((4, heads, rows, rows), F32),
             pltpu.VMEM((SLOTS, heads, rows, rows), BF16),
-            pltpu.VMEM((3, heads, 1, rows), F32),
+            pltpu.VMEM((4, heads, 1, rows), F32),
             pltpu.VMEM((heads, 8, rows), F32),
             pltpu.VMEM((heads, 1, rows), F32),
             pltpu.VMEM((heads, 8, rows), F32),

time: 54 us -> 54.1 us (level)
  no operation moved by 1% of the time
where the time goes in v5:
time: 54.1 us; the launch traced here: 54 us
  Pallas kernels  53.2 us (98%)
  between operations  0.8 us (1%)
    pallas_call x1, Pallas kernels, on_device(): pl.pallas_call(functools.partial(kernel, n_ctx, heads, rows, chunks), out...  52.2 us

profile of v5, /device:TPU:1, one launch (start us, length us, event | category | flops | bytes accessed | tf_op | source)
XLA Modules:
  0.0 54.0 jit_solution(10676836932993604741)
XLA Ops:
  0.6 52.2 %shard_map.93 = (bf16[256,1280]{1,0:T(8,128)(2,1)S(1)}, bf16[256,640]{1,0:T(8,128)(2,1)S(1)}, bf16[256,128]{1,0:T(8,128)(2,1)S(1)}, bf16[256,128]{1,0:T(8,128)(2,1)S(1)}) custom-call(s32[128]{0:T(128)} %doc_in.1, bf16[256,640]{1,0:T(8,128)(2,1)} %q_in.1, bf16[256,128]{1,0:T(8,128)(2,1)} %k_in.1, bf16[256,128]{1,0:T(8,128)(2,1)} %v_in.1, ...), custom_call_target="tpu_custom_call" | custom-call | tf_op jit(solution)/shard_map/pallas_call | solution.py:615
  52.8 1.0 %shard_map.94 = (bf16[256,1280]{1,0:T(8,128)(2,1)}, bf16[256,640]{1,0:T(8,128)(2,1)}, bf16[256,128]{1,0:T(8,128)(2,1)}, bf16[256,128]{1,0:T(8,128)(2,1)}) custom-call(bf16[256,1280]{1,0:T(8,128)(2,1)S(1)} %get-tuple-element.8.refs_0_, bf16[256,640]{1,0:T(8,128)(2,1)S(1)} %get-tuple-element.9.refs_1_, bf16[256,128]{1,0:T(8,128)(2,1)S(1)} %get-tuple-element.10.refs_2_, ...), custom_call_target="tpu_custom_call" | custom-call | tf_op jit(solution)/shard_map/pallas_call | solution.py:682
